TPU v7x, 32 devices: a whole 2x2x4 slice. The times are simulated.
32 devices in a mesh: seq: 16 (over z, y, x), head: 2 (over core).
Axes of the slice: x: 2, y: 2, z: 4, core: 2. Of those that a mesh axis runs over, the one named last changes fastest.
Arguments:
- tokens: bfloat16 [8192, 1280], P('seq'), may hold values from -40 to 40
- norm_gain: float32 [1280], replicated, may hold values from 0.1 to 1.9
- w_query: bfloat16 [1280, 1280], P(None, 'head'), may hold values from -1 to 1
- w_key: bfloat16 [1280, 1280], P(None, 'head'), may hold values from -1 to 1
- w_value: bfloat16 [1280, 1280], P(None, 'head'), may hold values from -0.15625 to 0.15625
- w_out: bfloat16 [1280, 1280], P('head'), may hold values from -0.15625 to 0.15625
- conv_in_w: bfloat16 [1280, 768], P(None, 'head'), may hold values from -0.15625 to 0.15625
- conv_gate_w: bfloat16 [1280, 768], P(None, 'head'), may hold values from -0.15625 to 0.15625
- conv_taps: bfloat16 [128, 768], P(None, 'head'), may hold values from -0.5 to 0.5
- conv_out_w: bfloat16 [768, 1280], P('head'), may hold values from -0.21875 to 0.21875
- chain_starts: int32 [12], replicated, may hold values from 0 to 7230, as said below
- block_lists: int32 [64, 4], P('seq'), may hold values from 0 to 63, as said below
- block_counts: int32 [64], P('seq'), may hold values from 0 to 4, as said below
Outputs:
- mixed: bfloat16 [8192, 1280], P(('seq', 'head'))
Inputs may be any that keep to these rules, and one draw needn't show every extreme that they name: chain_starts[0] is 0 and the starts increase; consecutive starts differ by 260 or more, and the last chain, which ends at token 8191, also has 260 tokens or more. `block_lists`: A shard is a run of 512 tokens. Every entry of row q, also past its count, names a key block in a shard one, two or three shards before or after the shard of query block q, never in that shard itself; the entries of one row are distinct. All rows of one query shard together name at most one block of any shard two or three shards away. Entries of row q of block_lists at slots block_counts[q] and beyond are not used.
All inputs are finite; a program needn't handle non-finite values.
Results may differ from a plain program's by a relative error of at most 0.012.
Values may be sent and summed in bfloat16 or wider, within the bound.
No kernel may reach another device: no remote copies, remote signals or barrier semaphores. Data moves between devices by JAX's collectives and lax.ppermute only.
A program may use at most 128 MiB of HBM per device.

v0:
```python
import functools
import math

import jax
import jax.numpy as jnp
from jax import lax
from jax.experimental import pallas as pl
from jax.experimental.pallas import tpu as pltpu
from jax.sharding import PartitionSpec as P


HD = 64
KTAP = 128
BLK = 128
HALF = 512
NB = 4
LANES = 128
AXES = ("seq", "head")
NEG = -1e30
F32 = jnp.float32
BF16 = jnp.bfloat16


def flat_pairs(count, target):
    pairs = []
    for i in range(count):
        for h in range(2):
            j = target(i, h)
            if 0 <= j < count:
                pairs.append((2 * i + h, 2 * j + h))
    return pairs


def swap(value):
    return lax.ppermute(value, "head", [(0, 1), (1, 0)])


def dot(a, b):
    return jnp.dot(a, b, preferred_element_type=F32)


SMEM = pl.BlockSpec(memory_space=pltpu.SMEM)
VMEM = pl.BlockSpec(memory_space=pltpu.VMEM)
ANY = pl.BlockSpec(memory_space=pl.ANY)


def limit(mib):
    return pltpu.CompilerParams(vmem_limit_bytes=mib << 20)


def in_hbm(value):
    return pltpu.with_memory_space_constraint(value, pltpu.HBM)


PIECES = 4


def plan_kernel(per_shard, nweights, lists_in, tokens, gain_in, *refs):
    weights, refs = refs[:nweights], refs[nweights:]
    mine, yours, normed, half, *refs = refs
    kept, (lists, gain, rows, sem) = refs[:nweights], refs[nweights:]
    me, core = lax.axis_index("seq"), lax.axis_index("head")
    size = tokens.shape[0] // PIECES
    copies = [
        pltpu.make_async_copy(
            tokens.at[pl.ds(n * size, size)], rows.at[pl.ds(n * size, size)], sem.at[n]
        )
        for n in range(PIECES)
    ]
    copies.append(pltpu.make_async_copy(lists_in, lists, sem.at[PIECES]))
    copies.append(pltpu.make_async_copy(gain_in, gain, sem.at[PIECES + 1]))
    for n in range(nweights):
        copies.append(pltpu.make_async_copy(weights[n], kept[n], sem.at[PIECES + 2 + n]))
    for copy in copies:
        copy.start()
    copies[PIECES + 1].wait()
    g = jnp.broadcast_to(gain[...].reshape(1, -1), (32, normed.shape[1]))

    def norm(r, c):
        here = pl.ds(pl.multiple_of(r * 32, 32), 32)
        x = rows[here, :].astype(F32)
        x = x * lax.rsqrt(jnp.mean(x * x, axis=1, keepdims=True) + 1e-05) * g
        normed[here, :] = x.astype(BF16)
        return c

    for n in range(PIECES):
        copies[n].wait()
        lax.fori_loop(n * size // 32, (n + 1) * size // 32, norm, 0)
    copies[PIECES].wait()

    def wanted(distance):
        low = (me + distance) * per_shard
        found = jnp.int32(0)
        for q in range(per_shard):
            for m in range(NB):
                local = lists[q, m] - low
                found = jnp.where((local >= 0) & (local < per_shard), local, found)
        return found

    side = 1 - 2 * core
    for n in range(2):
        mine[n] = wanted(side * (n + 2))
        yours[n] = wanted(-side * (n + 2))
    count = half.shape[0]
    half[...] = normed[pl.ds(pl.multiple_of(core * count, count), count), :]
    for copy in copies[PIECES + 2 :]:
        copy.wait()


def plan(lists, tokens, gain, weights):
    rows, cols = tokens.shape
    pair = jax.ShapeDtypeStruct((2,), jnp.int32)
    return pl.pallas_call(
        functools.partial(plan_kernel, rows // BLK, len(weights)),
        out_shape=[
            pair,
            pair,
            jax.ShapeDtypeStruct((rows, cols), BF16),
            jax.ShapeDtypeStruct((rows // 2, cols), BF16),
        ]
        + [jax.ShapeDtypeStruct(w.shape, BF16) for w in weights],
        in_specs=[ANY] * (3 + len(weights)),
        out_specs=[SMEM, SMEM] + [VMEM] * (2 + len(weights)),
        scratch_shapes=[
            pltpu.SMEM(lists.shape, jnp.int32),
            pltpu.VMEM(gain.shape, F32),
            pltpu.VMEM((rows, cols), BF16),
            pltpu.SemaphoreType.DMA((PIECES + 2 + len(weights),)),
        ],
        compiler_params=limit(14),
        name="plan",
    )(in_hbm(lists), in_hbm(tokens), in_hbm(gain), *[in_hbm(w) for w in weights])


def pick_own_kernel(asked, own, out):
    out[...] = own[pl.ds(pl.multiple_of(asked[0] * BLK, BLK), BLK), :]


def pick_other_kernel(asked, *refs):
    *parts, out = refs
    me, core = lax.axis_index("seq"), lax.axis_index("head")
    count = len(parts) // 2
    blocks = parts[0].shape[0] // BLK
    use_partner = (me % 2) == core
    slot = (asked[1] + core * (count * blocks // 2)) % (count * blocks)
    held = slot // blocks + jnp.where(use_partner, 0, count)
    here = pl.ds(pl.multiple_of((slot % blocks) * BLK, BLK), BLK)
    for k, ref in enumerate(parts):

        @pl.when(held == k)
        def _(ref=ref):
            out[...] = ref[here, :]


def pick(asked, sources):
    if len(sources) == 1:
        kernel = pick_own_kernel
    else:
        kernel = pick_other_kernel
    return pl.pallas_call(
        kernel,
        out_shape=jax.ShapeDtypeStruct((BLK, sources[0].shape[1]), BF16),
        in_specs=[SMEM] + [VMEM] * len(sources),
        out_specs=VMEM,
        compiler_params=limit(6),
        name="pick",
    )(asked, *sources)


def rim_rows(parts):
    mine, swapped = parts[len(parts) // 2 - 1], parts[-1]
    last = slice(mine.shape[0] - KTAP, mine.shape[0])
    return jnp.where(lax.axis_index("head") == 1, mine[last, :], swapped[last, :])


def own_kernel(scales, x_ref, *refs):
    count = len(scales)
    weights, outs = refs[:count], refs[count:]
    for n in range(count):
        y = dot(x_ref[...], weights[n][...])
        outs[n][...] = (y if scales[n] == 1.0 else y * scales[n]).astype(BF16)


def own_project(x, weights, scales):
    rows, cols = x.shape
    outs = [jax.ShapeDtypeStruct((rows, w.shape[1]), BF16) for w in weights]
    flops = sum(2 * rows * cols * w.shape[1] for w in weights)
    return pl.pallas_call(
        functools.partial(own_kernel, scales),
        out_shape=outs,
        in_specs=[VMEM] * (1 + len(weights)),
        out_specs=[VMEM] * len(outs),
        compiler_params=limit(14),
        cost_estimate=pl.CostEstimate(
            flops=flops, bytes_accessed=sum(w.size * 2 for w in weights), transcendentals=0
        ),
        name="own_project",
    )(x, *weights)


def other_kernel(*refs):
    *parts, wk, wv, wc, k_ref, v_ref, rim_ref = refs
    x = jnp.concatenate([part[...] for part in parts], axis=0)
    k_ref[...] = dot(x, wk[...]).astype(BF16)
    v_ref[...] = dot(x, wv[...]).astype(BF16)
    rim_ref[...] = dot(rim_rows(parts), wc[...]).astype(BF16)


def other_project(parts, wk, wv, wc):
    rows, cols = sum(part.shape[0] for part in parts), parts[0].shape[1]
    return pl.pallas_call(
        other_kernel,
        out_shape=[
            jax.ShapeDtypeStruct((rows, wk.shape[1]), BF16),
            jax.ShapeDtypeStruct((rows, wv.shape[1]), BF16),
            jax.ShapeDtypeStruct((KTAP, wc.shape[1]), BF16),
        ],
        in_specs=[VMEM] * (3 + len(parts)),
        out_specs=[VMEM] * 3,
        compiler_params=limit(10),
        cost_estimate=pl.CostEstimate(
            flops=4 * rows * cols * wk.shape[1], bytes_accessed=4 * wk.size, transcendentals=0
        ),
        name="other_project",
    )(*parts, wk, wv, wc)


BIG = 1 << 30
FAR = 1 << 20


def attention_kernel(
    first,
    fresh_parts,
    nch,
    per_shard,
    kblocks,
    starts,
    lists,
    counts,
    mine,
    yours,
    q_ref,
    *refs,
):
    k_in, v_in, *refs = refs
    new, (wk, wv, *refs) = refs[:fresh_parts], refs[fresh_parts:]
    if first:
        wc_in, o_ref, l_ref, mx_ref, rim_ref, *refs = refs
    else:
        o_ref, l_ref, mx_ref, g_ref, wo, wco, theirs, ours, *refs = refs
    k_all, v_all, qz, s_buf, bias, k_chain, i_chain, gblk, flag, ids, *refs = refs
    a_ref = None if first else refs[0]
    pairs = q_ref.shape[1] // LANES
    held = k_in.shape[0]
    k_all[:held] = k_in[...]
    v_all[:held] = v_in[...]
    fresh = jnp.concatenate([part[...] for part in new], axis=0)
    k_all[held:] = dot(fresh, wk[...]).astype(BF16)
    v_all[held:] = dot(fresh, wv[...]).astype(BF16)
    if first:
        rim_ref[...] = dot(rim_rows(new), wc_in[...]).astype(BF16)

    me, core = lax.axis_index("seq"), lax.axis_index("head")
    shards = lax.axis_size("seq")
    step = 1 - 2 * (me % 2)
    side = 1 - 2 * core
    turn = core * (per_shard // 2)
    own = me * per_shard

    def block_of(shard, local):
        return jnp.where((shard >= 0) & (shard < shards), shard * per_shard + local, -FAR)

    for p in range(per_shard):
        local = (turn + p) % per_shard
        if first:
            gblk[p] = own + p
            gblk[per_shard + p] = block_of(me + step, local)
        else:
            gblk[p] = block_of(me - step, local)
    if not first:
        for n in range(2):
            gblk[per_shard + 2 * n] = block_of(me + side * (n + 2), mine[n])
            gblk[per_shard + 2 * n + 1] = block_of(me - side * (n + 2), yours[n])

    def slot_of(block):
        shard = block // per_shard
        away = shard - me
        near_slot = (block % per_shard - turn) % per_shard
        if first:
            return jnp.where(away == step, per_shard + near_slot, kblocks)
        far_slot = per_shard + 2 * (jnp.abs(away) - 2) + jnp.where(away * side > 0, 0, 1)
        return jnp.where(
            away == -step, near_slot, jnp.where(jnp.abs(away) >= 2, far_slot, kblocks)
        )

    def chain_of(pos):
        return lax.fori_loop(
            0,
            nch,
            lambda c, n: n + jnp.where(starts[c] <= pos, 1, 0),
            jnp.full(pos.shape, -1, jnp.int32),
        )

    lane = lax.broadcasted_iota(jnp.int32, (BLK, LANES), 1)
    row = lax.broadcasted_iota(jnp.int32, (BLK, LANES), 0)
    low = lane < HD
    for b in range(kblocks):
        k_chain[pl.ds(b, 1), :] = gblk[b] * BLK + lane[0:1, :]
    k_chain[...] = chain_of(k_chain[...])
    bias[kblocks] = jnp.full((BLK, LANES), NEG, F32)

    def one_block(qb, carry):
        gq = own + qb
        q_first = gq * BLK
        q_last = q_first + BLK - 1

        def scan(c, found):
            begin, end, after = found
            s = starts[c]
            begin = jnp.where(s <= q_first, jnp.maximum(begin, s), begin)
            end = jnp.where(s > q_first, jnp.minimum(end, s), end)
            after = jnp.where(s > q_last, jnp.minimum(after, s), after)
            return begin, end, after

        begin, end, after = lax.fori_loop(
            0, nch, scan, (jnp.int32(0), jnp.int32(BIG), jnp.int32(BIG))
        )
        i_chain[...] = chain_of(q_first + row)
        zero = jnp.zeros((BLK, LANES), BF16)
        q_rows = pl.ds(pl.multiple_of(qb * BLK, BLK), BLK)
        for p in range(pairs):
            q = q_ref[q_rows, p * LANES : (p + 1) * LANES]
            qz[p, 0:BLK, :] = jnp.where(low, q, zero)
            qz[p, BLK : 2 * BLK, :] = jnp.where(low, zero, q)

        for b in range(kblocks + 1):
            flag[b] = 0

        def mark(m, c):
            flag[slot_of(lists[qb, m])] = 1
            return c

        lax.fori_loop(0, counts[qb], mark, 0)

        count = jnp.int32(0)
        for b in range(kblocks):
            gk = gblk[b]
            k_first = gk * BLK
            k_last = k_first + BLK - 1
            away = gk - gq
            near = (jnp.abs(away) * BLK <= HALF) & (k_last >= begin) & (k_first < after)
            listed = flag[b]
            one_chain = (k_first >= begin) & (jnp.maximum(k_last, q_last) < end)
            active = near | ((listed == 1) & jnp.logical_not(one_chain))
            ids[count] = b
            count = count + active.astype(jnp.int32)
            same = i_chain[...] == k_chain[b : b + 1, :]
            relative = away * BLK + lane - row
            in_window = jnp.where((relative >= -HALF) & (relative < HALF), 0.0, NEG)
            in_list = jnp.where(listed == 1, 0.0, NEG)
            bias[b] = jnp.where(same, in_window, in_list)
        ids[count] = kblocks
        ids[count + 1] = kblocks
        steps = jnp.maximum((count + 1) // 2, 1)

        def attend(steps):
            masks = [bias[ids[n]] for n in range(2 * steps)]
            rows_of = [
                pl.ds(pl.multiple_of(jnp.minimum(ids[n], kblocks - 1) * BLK, BLK), BLK)
                for n in range(2 * steps)
            ]
            for p in range(pairs):
                cols = slice(p * LANES, (p + 1) * LANES)
                if first:
                    m = None
                else:
                    old = mx_ref[q_rows, cols]
                    turned = pltpu.roll(old, HD, 1)
                    m = jnp.concatenate([jnp.where(low, old, turned), jnp.where(low, turned, old)], 0)
                for n in range(steps):
                    k = jnp.concatenate(
                        [k_all[rows_of[2 * n], cols], k_all[rows_of[2 * n + 1], cols]], axis=0
                    )
                    s = lax.dot_general(
                        qz[p], k, (((1,), (1,)), ((), ())), preferred_element_type=F32
                    )
                    mask = jnp.concatenate([masks[2 * n], masks[2 * n + 1]], axis=1)
                    s = s + jnp.concatenate([mask, mask], axis=0)
                    s_buf[p, n] = s
                    top = jnp.maximum(s[:, :LANES], s[:, LANES:])
                    m = top if m is None else jnp.maximum(m, top)
                m = jnp.broadcast_to(jnp.max(m, axis=1, keepdims=True), (2 * BLK, LANES))
                m2 = jnp.concatenate([m, m], axis=1)
                e = jnp.concatenate(
                    [jnp.exp2(s_buf[p, n] - m2).astype(BF16) for n in range(steps)], axis=1
                )
                v = jnp.concatenate([v_all[here, cols] for here in rows_of], axis=0)
                v = jnp.concatenate([v, jnp.ones_like(v)], axis=1)
                y = dot(e, v)
                o = jnp.where(low, y[:BLK, :LANES], y[BLK:, :LANES])
                l = jnp.where(low, y[:BLK, LANES:], y[BLK:, LANES:])
                m = jnp.where(low, m[:BLK], m[BLK:])
                if first:
                    o_ref[q_rows, cols] = o
                    l_ref[q_rows, cols] = l
                    mx_ref[q_rows, cols] = m
                else:
                    scale = jnp.exp2(old - m)
                    o = o + o_ref[q_rows, cols] * scale
                    l = l + l_ref[q_rows, cols] * scale
                    a_ref[q_rows, cols] = (o / l).astype(BF16)

        for n in range(1, kblocks // 2 + 1):

            @pl.when(steps == n)
            def _(n=n):
                attend(n)

        return carry

    lax.fori_loop(0, per_shard, one_block, 0)
    if not first:
        rows = ours.shape[0]
        for half, out in ((1 - core, theirs), (core, ours)):
            here = pl.ds(pl.multiple_of(half * rows, rows), rows)
            y = dot(a_ref[here, :], wo[...]) + dot(g_ref[here, :], wco[...])
            out[...] = y.astype(out.dtype)


def attention(context, queries, kv, new, weights, finish=None):
    rows, cols = queries.shape
    pairs = cols // LANES
    fresh = sum(part.shape[0] for part in new)
    keys = kv[0].shape[0] + fresh
    kblocks = keys // BLK
    steps = (kblocks + 1) // 2
    first = finish is None
    sums = jax.ShapeDtypeStruct((rows, cols), F32)
    if first:
        extra, more = (), []
        out_shape = [sums] * 3 + [jax.ShapeDtypeStruct((KTAP, weights[2].shape[1]), BF16)]
    else:
        extra, more = finish, [pltpu.VMEM((rows, cols), BF16)]
        wide = finish[4].shape[1]
        out_shape = [jax.ShapeDtypeStruct((rows // 2, wide), t) for t in (BF16, F32)]
    operands = (queries, *kv, *new, *weights, *extra)
    return pl.pallas_call(
        functools.partial(
            attention_kernel, first, len(new), context[0].shape[0], rows // BLK, kblocks
        ),
        out_shape=out_shape,
        in_specs=[SMEM] * len(context) + [VMEM] * len(operands),
        out_specs=[VMEM] * len(out_shape),
        scratch_shapes=[pltpu.VMEM((keys, cols), BF16)] * 2
        + [
            pltpu.VMEM((pairs, 2 * BLK, LANES), BF16),
            pltpu.VMEM((pairs, steps, 2 * BLK, 2 * BLK), F32),
            pltpu.VMEM((kblocks + 1, BLK, LANES), F32),
            pltpu.VMEM((kblocks, LANES), jnp.int32),
            pltpu.VMEM((BLK, LANES), jnp.int32),
            pltpu.SMEM((kblocks,), jnp.int32),
            pltpu.SMEM((kblocks + 1,), jnp.int32),
            pltpu.SMEM((kblocks + 2,), jnp.int32),
        ]
        + more,
        compiler_params=limit(32),
        cost_estimate=pl.CostEstimate(
            flops=4 * rows * keys * cols, bytes_accessed=4 * keys * cols, transcendentals=rows * keys
        ),
        name="attention",
    )(*context, *operands)


SEG = 8
KT = 8
JT = 16


def accumulate(accs, xv, wv):
    accs, taps = list(accs), len(wv)
    for n in range(taps):
        for j in range(len(accs)):
            accs[j] = accs[j] + xv[j - n + taps - 1] * wv[n]
    return tuple(accs)


def conv_kernel(
    nch, starts, own_ref, rim_p, rim_o, taps_ref, gate_ref, out_ref, x_ref, xs, ws, ms, y, x2, w2, y2
):
    rows, cols = own_ref.shape
    span = rows // SEG
    tiles = cols // LANES
    quarter, outs = KTAP // 4, span // 4
    me = lax.axis_index("seq")
    first = me * rows

    seg = lax.broadcasted_iota(jnp.int32, (SEG, LANES), 0)
    seg_first = first + seg * span

    def latest(c, found):
        begin, low = found
        s = starts[c]
        begin = jnp.where(s < seg_first + span, jnp.maximum(begin, s), begin)
        at = lax.rem(jnp.maximum(s - first, 0), span)
        inside = (s > first) & (s < first + rows) & (at > 0)
        return begin, jnp.where(inside, jnp.minimum(low, at), low)

    begin, low = lax.fori_loop(
        0, nch, latest, (jnp.zeros((SEG, LANES), jnp.int32), jnp.int32(span))
    )
    begin = begin - seg_first
    inner = begin > 0
    outer_begin = jnp.where(inner, -(1 << 30), begin)

    for t in range(tiles):
        cols_t = slice(t * LANES, (t + 1) * LANES)
        x_ref[t, 0:KTAP, :] = jnp.where(me % 2 == 1, rim_p[:, cols_t], rim_o[:, cols_t]).astype(F32)
        x_ref[t, pl.ds(KTAP, rows), :] = own_ref[:, cols_t].astype(F32)

    def row_of(j, t):
        v = x_ref[t, pl.ds(KTAP + j, SEG, stride=span), :]
        return jnp.where(j >= outer_begin, v, 0.0)

    def spread(n, before):
        j = 4 * (n - (quarter - 1))
        after = []
        for t in range(tiles):
            cols_t = slice(t * LANES, (t + 1) * LANES)
            a3, a2, a1 = before[3 * t : 3 * t + 3]
            b0, b1, b2, b3 = (row_of(j + k, t) for k in range(4))
            for s, (early, here, late) in enumerate(
                ((a1 - a2, b1 - b0, b3 - b2), (a2, b0, b2), (a2 - a3, b0 - a1, b2 - b1))
            ):
                xs[3 * s, n, :, cols_t] = late - here
                xs[3 * s + 1, n, :, cols_t] = here
                xs[3 * s + 2, n, :, cols_t] = here - early
            after += [b1, b2, b3]
        return tuple(after)

    start = 4 * (1 - quarter)
    lax.fori_loop(
        0,
        quarter - 1 + outs,
        spread,
        tuple(row_of(start + k, t) for t in range(tiles) for k in (-3, -2, -1)),
    )

    def widen(g, c):
        w = taps_ref[pl.ds(pl.multiple_of(g * 16, 16), 16), :].astype(F32)
        for r in range(4):
            w0, w1, w2, w3 = (w[4 * r + k : 4 * r + k + 1, :] for k in range(4))
            for s, (u, v) in enumerate(((w0, w2), (w0 + w1, w2 + w3), (w1, w3))):
                for k, value in enumerate((u, u + v, v)):
                    ws[3 * s + k, 4 * g + r] = jnp.broadcast_to(value, (SEG, cols))
        return c

    lax.fori_loop(0, KTAP // 16, widen, 0)

    for t in range(tiles):
        cols_t = slice(t * LANES, (t + 1) * LANES)

        def filtered(f, c, cols_t=cols_t):
            accs = tuple(jnp.zeros((SEG, LANES), F32) for _ in range(outs))
            for k0 in range(0, quarter, KT):
                at = quarter - k0 - KT
                xv = [xs[f, at + n, :, cols_t] for n in range(outs + KT - 1)]
                wv = [ws[f, k0 + n, :, cols_t] for n in range(KT)]
                accs = accumulate(accs, xv, wv)
            for j in range(outs):
                ms[f, j] = accs[j]
            return c

        lax.fori_loop(0, 9, filtered, 0)

        def join(b, c, cols_t=cols_t):
            odd, even = [], []
            for s in range(3):
                m0, m1, m2 = (ms[3 * s + k, b] for k in range(3))
                odd.append(m0 + m1)
                even.append(m1 - m2)
            for k, (m0, m1, m2) in enumerate((even, odd)):
                y[4 * b + 2 * k + 1, :, cols_t] = m0 + m1
                y[4 * b + 2 * k, :, cols_t] = m1 - m2
            return c

        lax.fori_loop(0, outs, join, 0)

    @pl.when(low < span)
    def _():
        pad = KT + JT
        x2[0:pad] = jnp.zeros((pad, SEG, cols), F32)

        def mask(j, c):
            for t in range(tiles):
                cols_t = slice(t * LANES, (t + 1) * LANES)
                v = x_ref[t, pl.ds(KTAP + j, SEG, stride=span), :]
                x2[pad + j, :, cols_t] = jnp.where(inner & (j >= begin), v, 0.0)
            return c

        lax.fori_loop(0, span, mask, 0)

        def widen2(g, c):
            w = taps_ref[pl.ds(pl.multiple_of(g * 16, 16), 16), :].astype(F32)
            for r in range(16):
                w2[16 * g + r] = jnp.broadcast_to(w[r : r + 1, :], (SEG, cols))
            return c

        lax.fori_loop(0, span // 16, widen2, 0)
        for t in range(tiles):
            cols_t = slice(t * LANES, (t + 1) * LANES)

            def outputs(jt, c, cols_t=cols_t):
                j0 = jt * JT

                def taps(g, accs):
                    k0 = g * KT
                    at = pad + j0 - k0 - (KT - 1)
                    xv = [x2[at + n, :, cols_t] for n in range(JT + KT - 1)]
                    wv = [w2[k0 + n, :, cols_t] for n in range(KT)]
                    return accumulate(accs, xv, wv)

                reach = j0 + JT - low
                accs = lax.fori_loop(
                    0,
                    (reach + KT - 1) // KT,
                    taps,
                    tuple(jnp.zeros((SEG, LANES), F32) for _ in range(JT)),
                )
                for j in range(JT):
                    here = y[j0 + j, :, cols_t]
                    y[j0 + j, :, cols_t] = jnp.where(inner & (j0 + j >= begin), accs[j], here)
                return c

            lax.fori_loop(low // JT, span // JT, outputs, 0)

    def collect(j, c):
        for t in range(tiles):
            cols_t = slice(t * LANES, (t + 1) * LANES)
            y2[t, pl.ds(j, SEG, stride=span), :] = y[j, :, cols_t]
        return c

    lax.fori_loop(0, span, collect, 0, unroll=4)

    def gating(r, c):
        at = pl.ds(pl.multiple_of(r * 64, 64), 64)
        for t in range(tiles):
            cols_t = slice(t * LANES, (t + 1) * LANES)
            g = gate_ref[at, cols_t].astype(F32)
            out_ref[at, cols_t] = (y2[t, at, :] * (g / (1.0 + jnp.exp(-g)))).astype(BF16)
        return c

    lax.fori_loop(0, rows // 64, gating, 0)


def convolution(starts, own, rim_p, rim_o, taps, gate):
    rows, cols = own.shape
    span = rows // SEG
    quarter, outs = KTAP // 4, span // 4
    tiles = cols // LANES
    return pl.pallas_call(
        functools.partial(conv_kernel, starts.shape[0]),
        out_shape=jax.ShapeDtypeStruct((rows, cols), BF16),
        in_specs=[SMEM] + [VMEM] * 5,
        out_specs=VMEM,
        scratch_shapes=[
            pltpu.VMEM((tiles, KTAP + rows, LANES), F32),
            pltpu.VMEM((9, quarter - 1 + outs, SEG, cols), F32),
            pltpu.VMEM((9, quarter, SEG, cols), F32),
            pltpu.VMEM((9, outs, SEG, LANES), F32),
            pltpu.VMEM((span, SEG, cols), F32),
            pltpu.VMEM((KT + JT + span, SEG, cols), F32),
            pltpu.VMEM((span, SEG, cols), F32),
            pltpu.VMEM((tiles, rows, LANES), F32),
        ],
        compiler_params=limit(20),
        cost_estimate=pl.CostEstimate(
            flops=40 * rows * cols * KTAP, bytes_accessed=8 * rows * cols, transcendentals=rows * cols
        ),
    )(starts, own, rim_p, rim_o, taps, gate)


def body(
    tokens,
    norm_gain,
    w_query,
    w_key,
    w_value,
    w_out,
    conv_in_w,
    conv_gate_w,
    conv_taps,
    conv_out_w,
    chain_starts,
    block_lists,
    block_counts,
):
    shards = lax.axis_size("seq")

    after = lax.optimization_barrier
    mine, yours, normed, half, w_query, w_key, w_value, conv_in_w, conv_gate_w = plan(
        block_lists, tokens, norm_gain, (w_query, w_key, w_value, conv_in_w, conv_gate_w)
    )
    to_asking = flat_pairs(shards, lambda i, h: i + (-2 if h == 0 else 2))
    to_asked = flat_pairs(shards, lambda i, h: i + (2 if h == 0 else -2))
    to_partner = flat_pairs(shards, lambda i, h: i ^ 1)
    to_other = flat_pairs(shards, lambda i, h: i + (2 if i % 2 == 0 else -2))
    chunks = [half[:BLK], half[BLK:]]
    partner, other = [None] * 2, [None] * 2
    for n in range(2):
        partner[n] = lax.ppermute(chunks[n], AXES, to_partner)
    asked = lax.ppermute(mine, AXES, to_asked)

    scale = math.log2(math.e) / math.sqrt(HD)
    queries, k_own, v_own = own_project(normed, (w_query, w_key, w_value), (scale, 1.0, 1.0))
    asked, k_own = after((asked, k_own))
    picked = pick(asked, (normed,))
    far = lax.ppermute(picked, AXES, to_asking)
    conv_input, conv_gate = own_project(normed, (conv_in_w, conv_gate_w), (1.0, 1.0))
    for n in range(2):
        other[n] = lax.ppermute(partner[n], AXES, to_other)
    partner += [swap(part) for part in partner]

    context = (chain_starts, block_lists, block_counts, mine, yours)
    *state, rim_p = attention(
        context, queries, (k_own, v_own), partner, (w_key, w_value, conv_in_w)
    )
    other, far, state = after((other, far, state))
    other += [swap(part) for part in other]
    far_s = swap(far)
    farther = lax.ppermute(pick(asked, (*partner, *other)), AXES, to_asking)

    k_o, v_o, rim_o = other_project(other, w_key, w_value, conv_in_w)
    gated = convolution(chain_starts, conv_input, rim_p, rim_o, conv_taps, conv_gate)
    farther, gated, k_o, v_o = after((farther, gated, k_o, v_o))
    theirs, ours = attention(
        context,
        queries,
        (k_o, v_o),
        (far, far_s, farther, swap(farther)),
        (w_key, w_value),
        (*state, gated, w_out, conv_out_w),
    )
    return (ours + swap(theirs).astype(F32)).astype(BF16)


def solution(mesh):
    return jax.shard_map(
        body,
        mesh=mesh,
        in_specs=(
            P("seq", None),
            P(),
            P(None, "head"),
            P(None, "head"),
            P(None, "head"),
            P("head", None),
            P(None, "head"),
            P(None, "head"),
            P(None, "head"),
            P("head", None),
            P(),
            P("seq", None),
            P("seq"),
        ),
        out_specs=P(("seq", "head"), None),
        check_vma=False,
    )
```

profile of v0, /device:TPU:21, one launch (start us, length us, event | category | flops | bytes accessed | tf_op | source)
XLA Modules:
  0.0 91.6 jit_solution(9866571651354652835)
XLA Ops:
  0.0 4.1 %plan.1 = (s32[2]{0:T(128)S(1)}, s32[2]{0:T(128)S(1)}, bf16[512,1280]{1,0:T(8,128)(2,1)S(1)}, bf16[256,1280]{1,0:T(8,128)(2,1)S(1)}, bf16[1280,640]{1,0:T(8,128)...) custom-call(s32[4,4]{1,0:T(4,128)} %lists.3, ...), custom_call_target="tpu_custom_call" | custom-call | tf_op jit(solution)/shard_map/plan/pallas_call | solution.py:113
  4.1 1.3 %collective-permute-start.2 = (bf16[128,1280]{1,0:T(8,128)(2,1)S(1)}, bf16[128,1280]{1,0:T(8,128)(2,1)S(1)}, u32[]{:S(2)}, u32[]{:S(2)}) collective-permute-start(bf16[128,1280]{1,0:T(8,128)(2,1)S(1)} %get-tuple-element.75), channel_id=1, source_target_pairs={{0,2},{1,3},{2,0},{3,1},{4,6},{5,7},{6,4},{7,5},{8,10},{9,11},{10,... | collective-permute-start | bytes 983048 | tf_op jit(solution)/shard_map/ppermute | solution.py:711
  5.4 0.3 collective-permute-start.1
  5.7 2.1 %collective-permute-start = (s32[2]{0:T(128)S(1)}, s32[2]{0:T(128)S(1)}, u32[]{:S(2)}, u32[]{:S(2)}) collective-permute-start(s32[2]{0:T(128)S(1)} %get-tuple-element.40.mine), channel_id=1, source_target_pairs={{0,4},{2,6},{4,8},{5,1},{6,10},{7,3},{8,12},{9,5},{10,14},{11,7},{... | collective-permute-start | bytes 32 | tf_op jit(solution)/shard_map/ppermute | solution.py:712
  7.8 5.0 %collective-permute-done.2.refs_3_.refs_1_ = bf16[128,1280]{1,0:T(8,128)(2,1)S(1)} collective-permute-done((bf16[128,1280]{1,0:T(8,128)(2,1)S(1)}, bf16[128,1280]{1,0:T(8,128)(2,1)S(1)}, u32[]{:S(2)}, u32[]{:S(2)}) %collective-permute-start.2) | collective-permute-done | bytes 327712 | tf_op jit(solution)/shard_map/ppermute | solution.py:711
  12.8 2.7 %collective-permute-start.4 = (bf16[128,1280]{1,0:T(8,128)(2,1)S(1)}, bf16[128,1280]{1,0:T(8,128)(2,1)S(1)}, u32[]{:S(2)}, u32[]{:S(2)}) collective-permute-start(bf16[128,1280]{1,0:T(8,128)(2,1)S(1)} %collective-permute-done.2.refs_3_.refs_1_), channel_id=1, source_target_pairs={{0,1},{1,0},{2,3},{3,2},{4,5},{5,4},{6,7},{7,6},{8,9},{9,8},{10,11... | collective-permute-start | bytes 983048 | tf_op jit(solution)/shard_map/ppermute | solution.py:35
  15.4 4.4 %collective-permute-done.1.refs_2_.refs_0_ = bf16[128,1280]{1,0:T(8,128)(2,1)S(1)} collective-permute-done((bf16[128,1280]{1,0:T(8,128)(2,1)S(1)}, bf16[128,1280]{1,0:T(8,128)(2,1)S(1)}, u32[]{:S(2)}, u32[]{:S(2)}) %collective-permute-start.1) | collective-permute-done | bytes 327712 | tf_op jit(solution)/shard_map/ppermute | solution.py:711
  19.8 1.5 %collective-permute-start.3 = (bf16[128,1280]{1,0:T(8,128)(2,1)S(1)}, bf16[128,1280]{1,0:T(8,128)(2,1)S(1)}, u32[]{:S(2)}, u32[]{:S(2)}) collective-permute-start(bf16[128,1280]{1,0:T(8,128)(2,1)S(1)} %collective-permute-done.1.refs_2_.refs_0_), channel_id=1, source_target_pairs={{0,1},{1,0},{2,3},{3,2},{4,5},{5,4},{6,7},{7,6},{8,9},{9,8},{10,11... | collective-permute-start | bytes 983048 | tf_op jit(solution)/shard_map/ppermute | solution.py:35
  21.3 3.2 %own_project.2 = (bf16[512,640]{1,0:T(8,128)(2,1)S(1)}, bf16[512,640]{1,0:T(8,128)(2,1)S(1)}, bf16[512,640]{1,0:T(8,128)(2,1)S(1)}) custom-call(bf16[512,1280]{1,0:T(8,128)(2,1)S(1)} %get-tuple-element.42.x_ref.own, bf16[1280,640]{1,0:T(8,128)(2,1)S(1)} %get-tuple-element.43.refs_0_, bf16[1280,640]{1,0:T(8,128)(2,1)S(1)} %get-tuple-element.44.refs_1_.refs_6_.refs_4_, ...), custom_call_target="tpu_custom_call" | custom-call | flops 2516582400 | bytes 4915200 | tf_op jit(solution)/shard_map/own_project/pallas_call | solution.py:188
  24.6 0.0 copy-start.2
  24.6 0.0 copy-start.3
  24.6 0.0 copy-start.4
  24.6 0.0 collective-permute-done.asked
  24.6 0.6 pick.2
  25.2 3.1 %collective-permute-start.7 = (bf16[128,1280]{1,0:T(8,128)(2,1)S(1)}, bf16[128,1280]{1,0:T(8,128)(2,1)S(1)}, u32[]{:S(2)}, u32[]{:S(2)}) collective-permute-start(bf16[128,1280]{1,0:T(8,128)(2,1)S(1)} %pick.2), channel_id=1, source_target_pairs={{1,5},{3,7},{4,0},{5,9},{6,2},{7,11},{8,4},{9,13},{10,6},{11,15},{... | collective-permute-start | bytes 983048 | tf_op jit(solution)/shard_map/ppermute | solution.py:718
  28.4 3.1 %collective-permute-start.6 = (bf16[128,1280]{1,0:T(8,128)(2,1)S(1)}, bf16[128,1280]{1,0:T(8,128)(2,1)S(1)}, u32[]{:S(2)}, u32[]{:S(2)}) collective-permute-start(bf16[128,1280]{1,0:T(8,128)(2,1)S(1)} %collective-permute-done.2.refs_3_.refs_1_), channel_id=1, source_target_pairs={{0,4},{1,5},{4,8},{5,9},{6,2},{7,3},{8,12},{9,13},{10,6},{11,7},{1... | collective-permute-start | bytes 983048 | tf_op jit(solution)/shard_map/ppermute | solution.py:721
  31.5 1.9 %collective-permute-start.5 = (bf16[128,1280]{1,0:T(8,128)(2,1)S(1)}, bf16[128,1280]{1,0:T(8,128)(2,1)S(1)}, u32[]{:S(2)}, u32[]{:S(2)}) collective-permute-start(bf16[128,1280]{1,0:T(8,128)(2,1)S(1)} %collective-permute-done.1.refs_2_.refs_0_), channel_id=1, source_target_pairs={{0,4},{1,5},{4,8},{5,9},{6,2},{7,3},{8,12},{9,13},{10,6},{11,7},{1... | collective-permute-start | bytes 983048 | tf_op jit(solution)/shard_map/ppermute | solution.py:721
  33.4 0.0 collective-permute-done.4.refs_5_.refs_3_
  33.5 0.0 collective-permute-done.3.refs_4_.refs_2_
  33.5 0.0 copy-done.2
  33.5 0.0 copy-done.3
  33.5 0.0 copy-done.4
  33.5 11.6 %attention.2 = (f32[512,640]{1,0:T(8,128)S(1)}, f32[512,640]{1,0:T(8,128)S(1)}, f32[512,640]{1,0:T(8,128)S(1)}, bf16[128,384]{1,0:T(8,128)(2,1)S(1)}) custom-call(s32[12]{0:T(128)S(1)} %copy-done.3, s32[4,4]{1,0:T(4,128)S(1)} %copy-done.2, s32[4]{0:T(128)S(1)} %copy-done.4, s32[2]{0:T(128)S(1)} %get-tuple-element.40.mine, s32[2]{0:T(128)S(1)} %get-tuple-element.41.yours, ...), custom_call_target="tpu_custom_call" | custom-call | flops 1342177280 | bytes 2621440 | tf_op jit(solution)/shard_map/attention/pallas_call | solution.py:448
  45.1 0.0 collective-permute-done.7.refs_2_
  45.1 0.8 collective-permute-done.6.refs_5_.refs_1_
  45.9 4.7 %collective-permute-done.5.refs_4_.refs_0_ = bf16[128,1280]{1,0:T(8,128)(2,1)S(1)} collective-permute-done((bf16[128,1280]{1,0:T(8,128)(2,1)S(1)}, bf16[128,1280]{1,0:T(8,128)(2,1)S(1)}, u32[]{:S(2)}, u32[]{:S(2)}) %collective-permute-start.5) | collective-permute-done | bytes 327712 | tf_op jit(solution)/shard_map/ppermute | solution.py:721
  50.6 0.0 collective-permute-start.8
  50.6 0.5 collective-permute-start.9
  51.1 1.1 %collective-permute-done.8.refs_6_.refs_2_ = bf16[128,1280]{1,0:T(8,128)(2,1)S(1)} collective-permute-done((bf16[128,1280]{1,0:T(8,128)(2,1)S(1)}, bf16[128,1280]{1,0:T(8,128)(2,1)S(1)}, u32[]{:S(2)}, u32[]{:S(2)}) %collective-permute-start.8) | collective-permute-done | bytes 327712 | tf_op jit(solution)/shard_map/ppermute | solution.py:35
  52.2 0.5 collective-permute-done.9.refs_7_.refs_3_
  52.7 0.6 pick.3
  53.3 4.1 %collective-permute-start.10 = (bf16[128,1280]{1,0:T(8,128)(2,1)S(1)}, bf16[128,1280]{1,0:T(8,128)(2,1)S(1)}, u32[]{:S(2)}, u32[]{:S(2)}) collective-permute-start(bf16[128,1280]{1,0:T(8,128)(2,1)S(1)} %pick.3), channel_id=1, source_target_pairs={{1,5},{3,7},{4,0},{5,9},{6,2},{7,11},{8,4},{9,13},{10,6},{11,15},{... | collective-permute-start | bytes 983048 | tf_op jit(solution)/shard_map/ppermute | solution.py:731
  57.4 1.5 %own_project.3 = (bf16[512,384]{1,0:T(8,128)(2,1)S(1)}, bf16[512,384]{1,0:T(8,128)(2,1)S(1)}) custom-call(bf16[512,1280]{1,0:T(8,128)(2,1)S(1)} %get-tuple-element.42.x_ref.own, bf16[1280,384]{1,0:T(8,128)(2,1)S(1)} %get-tuple-element.52.refs_8_.refs_0_.refs_6_, bf16[1280,384]{1,0:T(8,128)(2,1)S(1)} %get-tuple-element.58.refs_1_), custom_call_target="tpu_custom_call" | custom-call | flops 1006632960 | bytes 1966080 | tf_op jit(solution)/shard_map/own_project/pallas_call | solution.py:188
  59.0 0.0 copy-start.5
  59.0 0.1 collective-permute-start.11
  59.0 2.4 %other_project.1 = (bf16[512,640]{1,0:T(8,128)(2,1)S(1)}, bf16[512,640]{1,0:T(8,128)(2,1)S(1)}, bf16[128,384]{1,0:T(8,128)(2,1)S(1)}) custom-call(bf16[128,1280]{1,0:T(8,128)(2,1)S(1)} %collective-permute-done.5.refs_4_.refs_0_, bf16[128,1280]{1,0:T(8,128)(2,1)S(1)} %collective-permute-done.6.refs_5_.refs_1_, ...), custom_call_target="tpu_custom_call" | custom-call | flops 1677721600 | bytes 3276800 | tf_op jit(solution)/shard_map/other_project/pallas_call | solution.py:211
  61.5 0.0 copy-done.5
  61.5 0.0 copy-start
  61.5 0.0 copy-start.1
  61.5 12.4 %shard_map.127.refs_11_ = bf16[512,384]{1,0:T(8,128)(2,1)S(1)} custom-call(s32[12]{0:T(128)S(1)} %copy-done.3, bf16[512,384]{1,0:T(8,128)(2,1)S(1)} %get-tuple-element.59.own_ref, bf16[128,384]{1,0:T(8,128)(2,1)S(1)} %get-tuple-element.60.rim_p, bf16[128,384]{1,0:T(8,128)(2,1)S(1)} %get-tuple-element.61.rim_o, bf16[128,384]{1,0:T(8,128)(2,1)S(1)} %copy-done.5, ...), custom_call_target="tpu_custom_call" | custom-call | flops 1006632960 | bytes 1572864 | tf_op jit(solution)/shard_map/pallas_call | solution.py:661
  73.9 0.0 collective-permute-done.10.refs_4_
  73.9 0.6 collective-permute-start.12
  74.5 0.0 collective-permute-done.11.refs_3_
  74.5 1.3 %collective-permute-done.12.refs_5_ = bf16[128,1280]{1,0:T(8,128)(2,1)S(1)} collective-permute-done((bf16[128,1280]{1,0:T(8,128)(2,1)S(1)}, bf16[128,1280]{1,0:T(8,128)(2,1)S(1)}, u32[]{:S(2)}, u32[]{:S(2)}) %collective-permute-start.12) | collective-permute-done | bytes 327712 | tf_op jit(solution)/shard_map/ppermute | solution.py:35
  75.7 0.0 copy-done
  75.7 0.0 copy-done.1
  75.7 12.8 %attention.3 = (bf16[256,1280]{1,0:T(8,128)(2,1)S(1)}, f32[256,1280]{1,0:T(8,128)S(1)}) custom-call(s32[12]{0:T(128)S(1)} %copy-done.3, s32[4,4]{1,0:T(4,128)S(1)} %copy-done.2, s32[4]{0:T(128)S(1)} %copy-done.4, s32[2]{0:T(128)S(1)} %get-tuple-element.40.mine, s32[2]{0:T(128)S(1)} %get-tuple-element.41.yours, bf16[512,640]{1,0:T(8,128)(2,1)S(1)} %get-tuple-element.46.q_ref, ...), custom_call_target="tpu_custom_call" | custom-call | flops 1342177280 | bytes 2621440 | tf_op jit(solution)/shard_map/attention/pallas_call | solution.py:448
  88.5 0.4 collective-permute-start.13
  88.9 1.7 %collective-permute-done.13 = bf16[256,1280]{1,0:T(8,128)(2,1)S(1)} collective-permute-done((bf16[256,1280]{1,0:T(8,128)(2,1)S(1)}, bf16[256,1280]{1,0:T(8,128)(2,1)S(1)}, u32[]{:S(2)}, u32[]{:S(2)}) %collective-permute-start.13) | collective-permute-done | bytes 655392 | tf_op jit(solution)/shard_map/ppermute | solution.py:35
  90.7 1.0 %add_convert_fusion = bf16[256,1280]{1,0:T(8,128)(2,1)} fusion(f32[256,1280]{1,0:T(8,128)S(1)} %get-tuple-element.73, bf16[256,1280]{1,0:T(8,128)(2,1)S(1)} %collective-permute-done.13), kind=kLoop, calls=%fused_computation | loop fusion | flops 983040 | bytes 2621440 | tf_op jit(solution)/shard_map/convert_element_type | solution.py:744
  (1 shorter events, 0.0 us)
Async XLA Ops:
  4.1 8.7 %collective-permute-start.2 = (bf16[128,1280]{1,0:T(8,128)(2,1)S(1)}, bf16[128,1280]{1,0:T(8,128)(2,1)S(1)}, u32[]{:S(2)}, u32[]{:S(2)}) collective-permute-start(bf16[128,1280]{1,0:T(8,128)(2,1)S(1)} %get-tuple-element.75), channel_id=1, source_target_pairs={{0,2},{1,3},{2,0},{3,1},{4,6},{5,7},{6,4},{7,5},{8,10},{9,11},{10,... | collective-permute-start | bytes 983048 | tf_op jit(solution)/shard_map/ppermute | solution.py:711
  5.4 14.4 %collective-permute-start.1 = (bf16[128,1280]{1,0:T(8,128)(2,1)S(1)}, bf16[128,1280]{1,0:T(8,128)(2,1)S(1)}, u32[]{:S(2)}, u32[]{:S(2)}) collective-permute-start(bf16[128,1280]{1,0:T(8,128)(2,1)S(1)} %get-tuple-element.76), channel_id=1, source_target_pairs={{0,2},{1,3},{2,0},{3,1},{4,6},{5,7},{6,4},{7,5},{8,10},{9,11},{10,... | collective-permute-start | bytes 983048 | tf_op jit(solution)/shard_map/ppermute | solution.py:711
  5.7 19.0 %collective-permute-start = (s32[2]{0:T(128)S(1)}, s32[2]{0:T(128)S(1)}, u32[]{:S(2)}, u32[]{:S(2)}) collective-permute-start(s32[2]{0:T(128)S(1)} %get-tuple-element.40.mine), channel_id=1, source_target_pairs={{0,4},{2,6},{4,8},{5,1},{6,10},{7,3},{8,12},{9,5},{10,14},{11,7},{... | collective-permute-start | bytes 32 | tf_op jit(solution)/shard_map/ppermute | solution.py:712
  12.8 20.7 %collective-permute-start.4 = (bf16[128,1280]{1,0:T(8,128)(2,1)S(1)}, bf16[128,1280]{1,0:T(8,128)(2,1)S(1)}, u32[]{:S(2)}, u32[]{:S(2)}) collective-permute-start(bf16[128,1280]{1,0:T(8,128)(2,1)S(1)} %collective-permute-done.2.refs_3_.refs_1_), channel_id=1, source_target_pairs={{0,1},{1,0},{2,3},{3,2},{4,5},{5,4},{6,7},{7,6},{8,9},{9,8},{10,11... | collective-permute-start | bytes 983048 | tf_op jit(solution)/shard_map/ppermute | solution.py:35
  19.8 13.7 %collective-permute-start.3 = (bf16[128,1280]{1,0:T(8,128)(2,1)S(1)}, bf16[128,1280]{1,0:T(8,128)(2,1)S(1)}, u32[]{:S(2)}, u32[]{:S(2)}) collective-permute-start(bf16[128,1280]{1,0:T(8,128)(2,1)S(1)} %collective-permute-done.1.refs_2_.refs_0_), channel_id=1, source_target_pairs={{0,1},{1,0},{2,3},{3,2},{4,5},{5,4},{6,7},{7,6},{8,9},{9,8},{10,11... | collective-permute-start | bytes 983048 | tf_op jit(solution)/shard_map/ppermute | solution.py:35
  24.6 8.9 %copy-start.2 = (s32[4,4]{1,0:T(4,128)S(1)}, s32[4,4]{1,0:T(4,128)}, u32[]{:S(2)}) copy-start(s32[4,4]{1,0:T(4,128)} %lists.3) | copy-start | bytes 196
  24.6 8.9 %copy-start.3 = (s32[12]{0:T(128)S(1)}, s32[12]{0:T(128)}, u32[]{:S(2)}) copy-start(s32[12]{0:T(128)} %starts.5) | copy-start | bytes 148
  24.6 8.9 %copy-start.4 = (s32[4]{0:T(128)S(1)}, s32[4]{0:T(128)}, u32[]{:S(2)}) copy-start(s32[4]{0:T(128)} %counts.3) | copy-start | bytes 52
  25.2 19.9 %collective-permute-start.7 = (bf16[128,1280]{1,0:T(8,128)(2,1)S(1)}, bf16[128,1280]{1,0:T(8,128)(2,1)S(1)}, u32[]{:S(2)}, u32[]{:S(2)}) collective-permute-start(bf16[128,1280]{1,0:T(8,128)(2,1)S(1)} %pick.2), channel_id=1, source_target_pairs={{1,5},{3,7},{4,0},{5,9},{6,2},{7,11},{8,4},{9,13},{10,6},{11,15},{... | collective-permute-start | bytes 983048 | tf_op jit(solution)/shard_map/ppermute | solution.py:718
  28.4 17.5 %collective-permute-start.6 = (bf16[128,1280]{1,0:T(8,128)(2,1)S(1)}, bf16[128,1280]{1,0:T(8,128)(2,1)S(1)}, u32[]{:S(2)}, u32[]{:S(2)}) collective-permute-start(bf16[128,1280]{1,0:T(8,128)(2,1)S(1)} %collective-permute-done.2.refs_3_.refs_1_), channel_id=1, source_target_pairs={{0,4},{1,5},{4,8},{5,9},{6,2},{7,3},{8,12},{9,13},{10,6},{11,7},{1... | collective-permute-start | bytes 983048 | tf_op jit(solution)/shard_map/ppermute | solution.py:721
  31.5 19.1 %collective-permute-start.5 = (bf16[128,1280]{1,0:T(8,128)(2,1)S(1)}, bf16[128,1280]{1,0:T(8,128)(2,1)S(1)}, u32[]{:S(2)}, u32[]{:S(2)}) collective-permute-start(bf16[128,1280]{1,0:T(8,128)(2,1)S(1)} %collective-permute-done.1.refs_2_.refs_0_), channel_id=1, source_target_pairs={{0,4},{1,5},{4,8},{5,9},{6,2},{7,3},{8,12},{9,13},{10,6},{11,7},{1... | collective-permute-start | bytes 983048 | tf_op jit(solution)/shard_map/ppermute | solution.py:721
  50.6 1.6 %collective-permute-start.8 = (bf16[128,1280]{1,0:T(8,128)(2,1)S(1)}, bf16[128,1280]{1,0:T(8,128)(2,1)S(1)}, u32[]{:S(2)}, u32[]{:S(2)}) collective-permute-start(bf16[128,1280]{1,0:T(8,128)(2,1)S(1)} %collective-permute-done.5.refs_4_.refs_0_), channel_id=1, source_target_pairs={{0,1},{1,0},{2,3},{3,2},{4,5},{5,4},{6,7},{7,6},{8,9},{9,8},{10,11... | collective-permute-start | bytes 983048 | tf_op jit(solution)/shard_map/ppermute | solution.py:35
  50.6 2.1 %collective-permute-start.9 = (bf16[128,1280]{1,0:T(8,128)(2,1)S(1)}, bf16[128,1280]{1,0:T(8,128)(2,1)S(1)}, u32[]{:S(2)}, u32[]{:S(2)}) collective-permute-start(bf16[128,1280]{1,0:T(8,128)(2,1)S(1)} %collective-permute-done.6.refs_5_.refs_1_), channel_id=1, source_target_pairs={{0,1},{1,0},{2,3},{3,2},{4,5},{5,4},{6,7},{7,6},{8,9},{9,8},{10,11... | collective-permute-start | bytes 983048 | tf_op jit(solution)/shard_map/ppermute | solution.py:35
  53.3 20.6 %collective-permute-start.10 = (bf16[128,1280]{1,0:T(8,128)(2,1)S(1)}, bf16[128,1280]{1,0:T(8,128)(2,1)S(1)}, u32[]{:S(2)}, u32[]{:S(2)}) collective-permute-start(bf16[128,1280]{1,0:T(8,128)(2,1)S(1)} %pick.3), channel_id=1, source_target_pairs={{1,5},{3,7},{4,0},{5,9},{6,2},{7,11},{8,4},{9,13},{10,6},{11,15},{... | collective-permute-start | bytes 983048 | tf_op jit(solution)/shard_map/ppermute | solution.py:731
  59.0 2.5 %copy-start.5 = (bf16[128,384]{1,0:T(8,128)(2,1)S(1)}, bf16[128,384]{1,0:T(8,128)(2,1)}, u32[]{:S(2)}) copy-start(bf16[128,384]{1,0:T(8,128)(2,1)} %taps_ref.1) | copy-start | bytes 294916
  59.0 15.5 %collective-permute-start.11 = (bf16[128,1280]{1,0:T(8,128)(2,1)S(1)}, bf16[128,1280]{1,0:T(8,128)(2,1)S(1)}, u32[]{:S(2)}, u32[]{:S(2)}) collective-permute-start(bf16[128,1280]{1,0:T(8,128)(2,1)S(1)} %collective-permute-done.7.refs_2_), channel_id=1, source_target_pairs={{0,1},{1,0},{2,3},{3,2},{4,5},{5,4},{6,7},{7,6},{8,9},{9,8},{10,11... | collective-permute-start | bytes 983048 | tf_op jit(solution)/shard_map/ppermute | solution.py:35
  61.5 14.3 %copy-start = (bf16[640,1280]{1,0:T(8,128)(2,1)S(1)}, bf16[640,1280]{1,0:T(8,128)(2,1)}, u32[]{:S(2)}) copy-start(bf16[640,1280]{1,0:T(8,128)(2,1)} %refs_12_.1) | copy-start | bytes 4915204
  61.5 14.2 %copy-start.1 = (bf16[384,1280]{1,0:T(8,128)(2,1)S(1)}, bf16[384,1280]{1,0:T(8,128)(2,1)}, u32[]{:S(2)}) copy-start(bf16[384,1280]{1,0:T(8,128)(2,1)} %refs_13_.1) | copy-start | bytes 2949124
  73.9 1.8 %collective-permute-start.12 = (bf16[128,1280]{1,0:T(8,128)(2,1)S(1)}, bf16[128,1280]{1,0:T(8,128)(2,1)S(1)}, u32[]{:S(2)}, u32[]{:S(2)}) collective-permute-start(bf16[128,1280]{1,0:T(8,128)(2,1)S(1)} %collective-permute-done.10.refs_4_), channel_id=1, source_target_pairs={{0,1},{1,0},{2,3},{3,2},{4,5},{5,4},{6,7},{7,6},{8,9},{9,8},{10,11... | collective-permute-start | bytes 983048 | tf_op jit(solution)/shard_map/ppermute | solution.py:35
  88.5 2.2 %collective-permute-start.13 = (bf16[256,1280]{1,0:T(8,128)(2,1)S(1)}, bf16[256,1280]{1,0:T(8,128)(2,1)S(1)}, u32[]{:S(2)}, u32[]{:S(2)}) collective-permute-start(bf16[256,1280]{1,0:T(8,128)(2,1)S(1)} %get-tuple-element.74), channel_id=1, source_target_pairs={{0,1},{1,0},{2,3},{3,2},{4,5},{5,4},{6,7},{7,6},{8,9},{9,8},{10,11... | collective-permute-start | bytes 1966088 | tf_op jit(solution)/shard_map/ppermute | solution.py:35
where the time goes:
time: 91.8 us; the launch traced here: 91.6 us
  Pallas kernels  49.1 us (53%)
  starting transfers between devices  21.7 us (24%)
  waiting for transfers between devices  19.4 us (21%)
  other arithmetic  0.96 us (1%)
    pallas_call x2, Pallas kernels, attention(): pl.pallas_call(functools.partial(attention_kernel, first, len(new), conte...  24.3 us
    pallas_call x1, Pallas kernels, convolution(): pl.pallas_call(functools.partial(conv_kernel, starts.shape[0]), out_shape...  12.4 us
    ppermute x2, waiting for transfers between devices, body(): partner[n] = lax.ppermute(chunks[n], AXES, to_partner)  9.36 us
    ppermute x7, starting transfers between devices, swap(): return lax.ppermute(value, 'head', [(0, 1), (1, 0)])  5.77 us
    ppermute x2, waiting for transfers between devices, body(): other[n] = lax.ppermute(partner[n], AXES, to_other)  5.5 us
    ppermute x2, starting transfers between devices, body(): other[n] = lax.ppermute(partner[n], AXES, to_other)  5.07 us
    pallas_call x2, Pallas kernels, own_project(): pl.pallas_call(functools.partial(own_kernel, scales), out_shape=outs, in_...  4.77 us
    ppermute x7, waiting for transfers between devices, swap(): return lax.ppermute(value, 'head', [(0, 1), (1, 0)])  4.57 us
  transfers between devices with their start and end apart: 14, of which 8 were waited for; matrix products, arithmetic and copies ran while one was open for 0% of the time, Pallas kernels for 35%

commit v1 on v0

--- a/solution.py
+++ b/solution.py
@@ -173,20 +173,29 @@
     return jnp.where(lax.axis_index("head") == 1, mine[last, :], swapped[last, :])
 
 
-def own_kernel(scales, x_ref, *refs):
-    count = len(scales)
+def own_kernel(scale, x_ref, *refs):
+    count = len(refs) // 2
     weights, outs = refs[:count], refs[count:]
+    rows = x_ref.shape[0]
     for n in range(count):
         y = dot(x_ref[...], weights[n][...])
-        outs[n][...] = (y if scales[n] == 1.0 else y * scales[n]).astype(BF16)
-
-
-def own_project(x, weights, scales):
+        if n == 0 and scale is not None:
+            y = (y * scale).astype(BF16)
+            low = lax.broadcasted_iota(jnp.int32, y.shape, 1) % LANES < HD
+            outs[n][:rows, :] = jnp.where(low, y, jnp.zeros_like(y))
+            outs[n][rows:, :] = jnp.where(low, jnp.zeros_like(y), y)
+        else:
+            outs[n][...] = y.astype(BF16)
+
+
+def own_project(x, weights, scale=None):
     rows, cols = x.shape
     outs = [jax.ShapeDtypeStruct((rows, w.shape[1]), BF16) for w in weights]
+    if scale is not None:
+        outs[0] = jax.ShapeDtypeStruct((2 * rows, weights[0].shape[1]), BF16)
     flops = sum(2 * rows * cols * w.shape[1] for w in weights)
     return pl.pallas_call(
-        functools.partial(own_kernel, scales),
+        functools.partial(own_kernel, scale),
         out_shape=outs,
         in_specs=[VMEM] * (1 + len(weights)),
         out_specs=[VMEM] * len(outs),
@@ -199,30 +208,25 @@
 
 
 def other_kernel(*refs):
-    *parts, wk, wv, wc, k_ref, v_ref, rim_ref = refs
+    *parts, wk, wv, k_ref, v_ref = refs
     x = jnp.concatenate([part[...] for part in parts], axis=0)
     k_ref[...] = dot(x, wk[...]).astype(BF16)
     v_ref[...] = dot(x, wv[...]).astype(BF16)
-    rim_ref[...] = dot(rim_rows(parts), wc[...]).astype(BF16)
-
-
-def other_project(parts, wk, wv, wc):
+
+
+def other_project(parts, wk, wv):
     rows, cols = sum(part.shape[0] for part in parts), parts[0].shape[1]
     return pl.pallas_call(
         other_kernel,
-        out_shape=[
-            jax.ShapeDtypeStruct((rows, wk.shape[1]), BF16),
-            jax.ShapeDtypeStruct((rows, wv.shape[1]), BF16),
-            jax.ShapeDtypeStruct((KTAP, wc.shape[1]), BF16),
-        ],
-        in_specs=[VMEM] * (3 + len(parts)),
-        out_specs=[VMEM] * 3,
+        out_shape=[jax.ShapeDtypeStruct((rows, w.shape[1]), BF16) for w in (wk, wv)],
+        in_specs=[VMEM] * (2 + len(parts)),
+        out_specs=[VMEM] * 2,
         compiler_params=limit(10),
         cost_estimate=pl.CostEstimate(
             flops=4 * rows * cols * wk.shape[1], bytes_accessed=4 * wk.size, transcendentals=0
         ),
         name="other_project",
-    )(*parts, wk, wv, wc)
+    )(*parts, wk, wv)
 
 
 BIG = 1 << 30
@@ -249,7 +253,7 @@
         wc_in, o_ref, l_ref, mx_ref, rim_ref, *refs = refs
     else:
         o_ref, l_ref, mx_ref, g_ref, wo, wco, theirs, ours, *refs = refs
-    k_all, v_all, qz, s_buf, bias, k_chain, i_chain, gblk, flag, ids, *refs = refs
+    k_all, v_all, s_buf, m_buf, bias, k_chain, i_chain, gblk, flag, ids, around, *refs = refs
     a_ref = None if first else refs[0]
     pairs = q_ref.shape[1] // LANES
     held = k_in.shape[0]
@@ -310,29 +314,32 @@
     k_chain[...] = chain_of(k_chain[...])
     bias[kblocks] = jnp.full((BLK, LANES), NEG, F32)
 
+    def scan(c, found):
+        s, out = starts[c], []
+        for n in range(per_shard):
+            q_first = (own + n) * BLK
+            chain, begin, end, after = found[4 * n : 4 * n + 4]
+            ahead = s <= q_first
+            out += [
+                chain + ahead.astype(jnp.int32),
+                jnp.where(ahead, jnp.maximum(begin, s), begin),
+                jnp.where(ahead, end, jnp.minimum(end, s)),
+                jnp.where(s > q_first + BLK - 1, jnp.minimum(after, s), after),
+            ]
+        return tuple(out)
+
+    none = (jnp.int32(-1), jnp.int32(0), jnp.int32(BIG), jnp.int32(BIG))
+    for n, value in enumerate(lax.fori_loop(0, nch, scan, none * per_shard)):
+        around[n] = value
+
     def one_block(qb, carry):
         gq = own + qb
         q_first = gq * BLK
         q_last = q_first + BLK - 1
-
-        def scan(c, found):
-            begin, end, after = found
-            s = starts[c]
-            begin = jnp.where(s <= q_first, jnp.maximum(begin, s), begin)
-            end = jnp.where(s > q_first, jnp.minimum(end, s), end)
-            after = jnp.where(s > q_last, jnp.minimum(after, s), after)
-            return begin, end, after
-
-        begin, end, after = lax.fori_loop(
-            0, nch, scan, (jnp.int32(0), jnp.int32(BIG), jnp.int32(BIG))
-        )
-        i_chain[...] = chain_of(q_first + row)
-        zero = jnp.zeros((BLK, LANES), BF16)
+        chain, begin, end, after = (around[4 * qb + n] for n in range(4))
+        i_chain[...] = jnp.where(q_first + row >= end, chain + 1, chain)
         q_rows = pl.ds(pl.multiple_of(qb * BLK, BLK), BLK)
-        for p in range(pairs):
-            q = q_ref[q_rows, p * LANES : (p + 1) * LANES]
-            qz[p, 0:BLK, :] = jnp.where(low, q, zero)
-            qz[p, BLK : 2 * BLK, :] = jnp.where(low, zero, q)
+        q_rows_high = pl.ds(pl.multiple_of((per_shard + qb) * BLK, BLK), BLK)
 
         for b in range(kblocks + 1):
             flag[b] = 0
@@ -356,6 +363,9 @@
             ids[count] = b
             count = count + active.astype(jnp.int32)
             same = i_chain[...] == k_chain[b : b + 1, :]
+            if first and b < per_shard:
+                bias[b] = jnp.where(same, 0.0, NEG)
+                continue
             relative = away * BLK + lane - row
             in_window = jnp.where((relative >= -HALF) & (relative < HALF), 0.0, NEG)
             in_list = jnp.where(listed == 1, 0.0, NEG)
@@ -370,7 +380,8 @@
                 pl.ds(pl.multiple_of(jnp.minimum(ids[n], kblocks - 1) * BLK, BLK), BLK)
                 for n in range(2 * steps)
             ]
-            for p in range(pairs):
+
+            def scores(p):
                 cols = slice(p * LANES, (p + 1) * LANES)
                 if first:
                     m = None
@@ -378,19 +389,24 @@
                     old = mx_ref[q_rows, cols]
                     turned = pltpu.roll(old, HD, 1)
                     m = jnp.concatenate([jnp.where(low, old, turned), jnp.where(low, turned, old)], 0)
+                q = jnp.concatenate([q_ref[q_rows, cols], q_ref[q_rows_high, cols]], axis=0)
                 for n in range(steps):
                     k = jnp.concatenate(
                         [k_all[rows_of[2 * n], cols], k_all[rows_of[2 * n + 1], cols]], axis=0
                     )
                     s = lax.dot_general(
-                        qz[p], k, (((1,), (1,)), ((), ())), preferred_element_type=F32
+                        q, k, (((1,), (1,)), ((), ())), preferred_element_type=F32
                     )
                     mask = jnp.concatenate([masks[2 * n], masks[2 * n + 1]], axis=1)
                     s = s + jnp.concatenate([mask, mask], axis=0)
                     s_buf[p, n] = s
                     top = jnp.maximum(s[:, :LANES], s[:, LANES:])
                     m = top if m is None else jnp.maximum(m, top)
-                m = jnp.broadcast_to(jnp.max(m, axis=1, keepdims=True), (2 * BLK, LANES))
+                m_buf[p] = jnp.broadcast_to(jnp.max(m, axis=1, keepdims=True), (2 * BLK, LANES))
+
+            def sums(p):
+                cols = slice(p * LANES, (p + 1) * LANES)
+                m = m_buf[p]
                 m2 = jnp.concatenate([m, m], axis=1)
                 e = jnp.concatenate(
                     [jnp.exp2(s_buf[p, n] - m2).astype(BF16) for n in range(steps)], axis=1
@@ -406,10 +422,16 @@
                     l_ref[q_rows, cols] = l
                     mx_ref[q_rows, cols] = m
                 else:
-                    scale = jnp.exp2(old - m)
+                    scale = jnp.exp2(mx_ref[q_rows, cols] - m)
                     o = o + o_ref[q_rows, cols] * scale
                     l = l + l_ref[q_rows, cols] * scale
                     a_ref[q_rows, cols] = (o / l).astype(BF16)
+
+            scores(0)
+            for p in range(pairs):
+                if p + 1 < pairs:
+                    scores(p + 1)
+                sums(p)
 
         for n in range(1, kblocks // 2 + 1):
 
@@ -429,7 +451,7 @@
 
 
 def attention(context, queries, kv, new, weights, finish=None):
-    rows, cols = queries.shape
+    rows, cols = kv[0].shape
     pairs = cols // LANES
     fresh = sum(part.shape[0] for part in new)
     keys = kv[0].shape[0] + fresh
@@ -454,14 +476,15 @@
         out_specs=[VMEM] * len(out_shape),
         scratch_shapes=[pltpu.VMEM((keys, cols), BF16)] * 2
         + [
-            pltpu.VMEM((pairs, 2 * BLK, LANES), BF16),
             pltpu.VMEM((pairs, steps, 2 * BLK, 2 * BLK), F32),
+            pltpu.VMEM((pairs, 2 * BLK, LANES), F32),
             pltpu.VMEM((kblocks + 1, BLK, LANES), F32),
             pltpu.VMEM((kblocks, LANES), jnp.int32),
             pltpu.VMEM((BLK, LANES), jnp.int32),
             pltpu.SMEM((kblocks,), jnp.int32),
             pltpu.SMEM((kblocks + 1,), jnp.int32),
             pltpu.SMEM((kblocks + 2,), jnp.int32),
+            pltpu.SMEM((4 * rows // BLK,), jnp.int32),
         ]
         + more,
         compiler_params=limit(32),
@@ -474,7 +497,6 @@
 
 SEG = 8
 KT = 8
-JT = 16
 
 
 def accumulate(accs, xv, wv):
@@ -486,7 +508,7 @@
 
 
 def conv_kernel(
-    nch, starts, own_ref, rim_p, rim_o, taps_ref, gate_ref, out_ref, x_ref, xs, ws, ms, y, x2, w2, y2
+    nch, starts, own_ref, rim_p, last, last_s, wc, taps_ref, gate_ref, out_ref, x_ref, xs, ws, ms, y, xl, tf, y2
 ):
     rows, cols = own_ref.shape
     span = rows // SEG
@@ -498,25 +520,21 @@
     seg = lax.broadcasted_iota(jnp.int32, (SEG, LANES), 0)
     seg_first = first + seg * span
 
-    def latest(c, found):
-        begin, low = found
+    def latest(c, begin):
         s = starts[c]
-        begin = jnp.where(s < seg_first + span, jnp.maximum(begin, s), begin)
-        at = lax.rem(jnp.maximum(s - first, 0), span)
-        inside = (s > first) & (s < first + rows) & (at > 0)
-        return begin, jnp.where(inside, jnp.minimum(low, at), low)
-
-    begin, low = lax.fori_loop(
-        0, nch, latest, (jnp.zeros((SEG, LANES), jnp.int32), jnp.int32(span))
-    )
+        return jnp.where(s < seg_first + span, jnp.maximum(begin, s), begin)
+
+    begin = lax.fori_loop(0, nch, latest, jnp.zeros((SEG, LANES), jnp.int32))
     begin = begin - seg_first
     inner = begin > 0
     outer_begin = jnp.where(inner, -(1 << 30), begin)
 
+    rim_o = dot(rim_rows((last, last_s)), wc[...]).astype(BF16)
     for t in range(tiles):
         cols_t = slice(t * LANES, (t + 1) * LANES)
         x_ref[t, 0:KTAP, :] = jnp.where(me % 2 == 1, rim_p[:, cols_t], rim_o[:, cols_t]).astype(F32)
         x_ref[t, pl.ds(KTAP, rows), :] = own_ref[:, cols_t].astype(F32)
+        x_ref[t, pl.ds(KTAP + rows, 8), :] = jnp.zeros((8, LANES), F32)
 
     def row_of(j, t):
         v = x_ref[t, pl.ds(KTAP + j, SEG, stride=span), :]
@@ -541,13 +559,17 @@
     start = 4 * (1 - quarter)
     lax.fori_loop(
         0,
-        quarter - 1 + outs,
+        quarter + outs,
         spread,
         tuple(row_of(start + k, t) for t in range(tiles) for k in (-3, -2, -1)),
+        unroll=2,
     )
 
     def widen(g, c):
-        w = taps_ref[pl.ds(pl.multiple_of(g * 16, 16), 16), :].astype(F32)
+        here = pl.ds(pl.multiple_of(g * 16, 16), 16)
+        w = taps_ref[here, :].astype(F32)
+        for t in range(tiles):
+            tf[t, here, :] = w[:, t * LANES : (t + 1) * LANES]
         for r in range(4):
             w0, w1, w2, w3 = (w[4 * r + k : 4 * r + k + 1, :] for k in range(4))
             for s, (u, v) in enumerate(((w0, w2), (w0 + w1, w2 + w3), (w1, w3))):
@@ -586,54 +608,6 @@
 
         lax.fori_loop(0, outs, join, 0)
 
-    @pl.when(low < span)
-    def _():
-        pad = KT + JT
-        x2[0:pad] = jnp.zeros((pad, SEG, cols), F32)
-
-        def mask(j, c):
-            for t in range(tiles):
-                cols_t = slice(t * LANES, (t + 1) * LANES)
-                v = x_ref[t, pl.ds(KTAP + j, SEG, stride=span), :]
-                x2[pad + j, :, cols_t] = jnp.where(inner & (j >= begin), v, 0.0)
-            return c
-
-        lax.fori_loop(0, span, mask, 0)
-
-        def widen2(g, c):
-            w = taps_ref[pl.ds(pl.multiple_of(g * 16, 16), 16), :].astype(F32)
-            for r in range(16):
-                w2[16 * g + r] = jnp.broadcast_to(w[r : r + 1, :], (SEG, cols))
-            return c
-
-        lax.fori_loop(0, span // 16, widen2, 0)
-        for t in range(tiles):
-            cols_t = slice(t * LANES, (t + 1) * LANES)
-
-            def outputs(jt, c, cols_t=cols_t):
-                j0 = jt * JT
-
-                def taps(g, accs):
-                    k0 = g * KT
-                    at = pad + j0 - k0 - (KT - 1)
-                    xv = [x2[at + n, :, cols_t] for n in range(JT + KT - 1)]
-                    wv = [w2[k0 + n, :, cols_t] for n in range(KT)]
-                    return accumulate(accs, xv, wv)
-
-                reach = j0 + JT - low
-                accs = lax.fori_loop(
-                    0,
-                    (reach + KT - 1) // KT,
-                    taps,
-                    tuple(jnp.zeros((SEG, LANES), F32) for _ in range(JT)),
-                )
-                for j in range(JT):
-                    here = y[j0 + j, :, cols_t]
-                    y[j0 + j, :, cols_t] = jnp.where(inner & (j0 + j >= begin), accs[j], here)
-                return c
-
-            lax.fori_loop(low // JT, span // JT, outputs, 0)
-
     def collect(j, c):
         for t in range(tiles):
             cols_t = slice(t * LANES, (t + 1) * LANES)
@@ -641,6 +615,47 @@
         return c
 
     lax.fori_loop(0, span, collect, 0, unroll=4)
+
+    eighth = span // SEG
+    xl[:, 0:span, :] = jnp.zeros((tiles, span, LANES), F32)
+    row_in = lax.broadcasted_iota(jnp.int32, (span, LANES), 0)
+
+    def repair(c, carry):
+        at = starts[c] - first
+        seg_at, from_row = at // span, lax.rem(at, span)
+
+        @pl.when((at > 0) & (at < rows) & (from_row > 0))
+        def _():
+            base = pl.multiple_of(seg_at * span, span)
+            for t in range(tiles):
+                x = x_ref[t, pl.ds(KTAP + base, span), :]
+                xl[t, span:, :] = jnp.where(row_in >= from_row, x, 0.0)
+            for t in range(tiles):
+
+                def taps(g, accs, t=t):
+                    k0 = pl.multiple_of(g * KT, KT)
+                    lo = span - k0 - (KT - 1)
+                    xv = [
+                        xl[t, pl.ds(lo + n, SEG, stride=eighth), :] for n in range(eighth + KT - 1)
+                    ]
+                    w = tf[t, pl.ds(k0, KT), :]
+                    wv = [jnp.broadcast_to(w[n : n + 1, :], (SEG, LANES)) for n in range(KT)]
+                    return accumulate(accs, xv, wv)
+
+                accs = lax.fori_loop(
+                    0,
+                    (span - from_row + KT - 1) // KT,
+                    taps,
+                    tuple(jnp.zeros((SEG, LANES), F32) for _ in range(eighth)),
+                )
+                part = lax.broadcasted_iota(jnp.int32, (SEG, LANES), 0) * eighth
+                for j in range(eighth):
+                    here = pl.ds(base + j, SEG, stride=eighth)
+                    y2[t, here, :] = jnp.where(part + j >= from_row, accs[j], y2[t, here, :])
+
+        return carry
+
+    lax.fori_loop(0, nch, repair, 0)
 
     def gating(r, c):
         at = pl.ds(pl.multiple_of(r * 64, 64), 64)
@@ -653,7 +668,7 @@
     lax.fori_loop(0, rows // 64, gating, 0)
 
 
-def convolution(starts, own, rim_p, rim_o, taps, gate):
+def convolution(starts, own, rim_p, last, last_s, wc, taps, gate):
     rows, cols = own.shape
     span = rows // SEG
     quarter, outs = KTAP // 4, span // 4
@@ -661,23 +676,23 @@
     return pl.pallas_call(
         functools.partial(conv_kernel, starts.shape[0]),
         out_shape=jax.ShapeDtypeStruct((rows, cols), BF16),
-        in_specs=[SMEM] + [VMEM] * 5,
+        in_specs=[SMEM] + [VMEM] * 7,
         out_specs=VMEM,
         scratch_shapes=[
-            pltpu.VMEM((tiles, KTAP + rows, LANES), F32),
-            pltpu.VMEM((9, quarter - 1 + outs, SEG, cols), F32),
+            pltpu.VMEM((tiles, KTAP + rows + 8, LANES), F32),
+            pltpu.VMEM((9, quarter + outs, SEG, cols), F32),
             pltpu.VMEM((9, quarter, SEG, cols), F32),
             pltpu.VMEM((9, outs, SEG, LANES), F32),
             pltpu.VMEM((span, SEG, cols), F32),
-            pltpu.VMEM((KT + JT + span, SEG, cols), F32),
-            pltpu.VMEM((span, SEG, cols), F32),
+            pltpu.VMEM((tiles, 2 * span, LANES), F32),
+            pltpu.VMEM((tiles, KTAP, LANES), F32),
             pltpu.VMEM((tiles, rows, LANES), F32),
         ],
         compiler_params=limit(20),
         cost_estimate=pl.CostEstimate(
             flops=40 * rows * cols * KTAP, bytes_accessed=8 * rows * cols, transcendentals=rows * cols
         ),
-    )(starts, own, rim_p, rim_o, taps, gate)
+    )(starts, own, rim_p, last, last_s, wc, taps, gate)
 
 
 def body(
@@ -712,11 +727,11 @@
     asked = lax.ppermute(mine, AXES, to_asked)
 
     scale = math.log2(math.e) / math.sqrt(HD)
-    queries, k_own, v_own = own_project(normed, (w_query, w_key, w_value), (scale, 1.0, 1.0))
+    queries, k_own, v_own = own_project(normed, (w_query, w_key, w_value), scale)
     asked, k_own = after((asked, k_own))
     picked = pick(asked, (normed,))
     far = lax.ppermute(picked, AXES, to_asking)
-    conv_input, conv_gate = own_project(normed, (conv_in_w, conv_gate_w), (1.0, 1.0))
+    conv_input, conv_gate = own_project(normed, (conv_in_w, conv_gate_w))
     for n in range(2):
         other[n] = lax.ppermute(partner[n], AXES, to_other)
     partner += [swap(part) for part in partner]
@@ -730,14 +745,17 @@
     far_s = swap(far)
     farther = lax.ppermute(pick(asked, (*partner, *other)), AXES, to_asking)
 
-    k_o, v_o, rim_o = other_project(other, w_key, w_value, conv_in_w)
-    gated = convolution(chain_starts, conv_input, rim_p, rim_o, conv_taps, conv_gate)
-    farther, gated, k_o, v_o = after((farther, gated, k_o, v_o))
+    gated = convolution(
+        chain_starts, conv_input, rim_p, other[1], other[3], conv_in_w, conv_taps, conv_gate
+    )
+    farther, gated, other = after((farther, gated, other))
+    farther_s = swap(farther)
+    k_o, v_o = other_project(other, w_key, w_value)
     theirs, ours = attention(
         context,
         queries,
         (k_o, v_o),
-        (far, far_s, farther, swap(farther)),
+        (far, far_s, farther, farther_s),
         (w_key, w_value),
         (*state, gated, w_out, conv_out_w),
     )

time: 91.8 us -> 86.9 us (0.947)
  the two profiles are of different devices: /device:TPU:21 before, /device:TPU:15 now
where the time goes in v1:
time: 86.9 us; the launch traced here: 86.2 us
  Pallas kernels  43.4 us (50%)
  starting transfers between devices  21.5 us (25%)
  waiting for transfers between devices  20 us (23%)
  other arithmetic  0.96 us (1%)
    pallas_call x2, Pallas kernels, attention(): pl.pallas_call(functools.partial(attention_kernel, first, len(new), conte...  21.6 us
    pallas_call x1, Pallas kernels, convolution(): pl.pallas_call(functools.partial(conv_kernel, starts.shape[0]), out_shape...  9.56 us
    ppermute x2, waiting for transfers between devices, body(): partner[n] = lax.ppermute(chunks[n], AXES, to_partner)  9.36 us
    ppermute x1, waiting for transfers between devices, body(): far = lax.ppermute(picked, AXES, to_asking)  6.97 us
    ppermute x7, starting transfers between devices, swap(): return lax.ppermute(value, 'head', [(0, 1), (1, 0)])  5.41 us
    ppermute x2, starting transfers between devices, body(): other[n] = lax.ppermute(partner[n], AXES, to_other)  5.17 us
    pallas_call x2, Pallas kernels, own_project(): pl.pallas_call(functools.partial(own_kernel, scale), out_shape=outs, in_s...  4.77 us
    ppermute x1, starting transfers between devices, body(): farther = lax.ppermute(pick(asked, (*partner, *other)), AXES, to_asking)  4.1 us
  transfers between devices with their start and end apart: 14, of which 6 were waited for; matrix products, arithmetic and copies ran while one was open for 0% of the time, Pallas kernels for 31%

profile of v1, /device:TPU:15, one launch (start us, length us, event | category | flops | bytes accessed | tf_op | source)
XLA Modules:
  0.0 86.2 jit_solution(10134082980129165613)
XLA Ops:
  0.0 4.1 %plan.1 = (s32[2]{0:T(128)S(1)}, s32[2]{0:T(128)S(1)}, bf16[512,1280]{1,0:T(8,128)(2,1)S(1)}, bf16[256,1280]{1,0:T(8,128)(2,1)S(1)}, bf16[1280,640]{1,0:T(8,128)...) custom-call(s32[4,4]{1,0:T(4,128)} %lists.3, ...), custom_call_target="tpu_custom_call" | custom-call | tf_op jit(solution)/shard_map/plan/pallas_call | solution.py:113
  4.1 0.3 collective-permute-start.2
  4.4 1.2 %collective-permute-start.1 = (bf16[128,1280]{1,0:T(8,128)(2,1)S(1)}, bf16[128,1280]{1,0:T(8,128)(2,1)S(1)}, u32[]{:S(2)}, u32[]{:S(2)}) collective-permute-start(bf16[128,1280]{1,0:T(8,128)(2,1)S(1)} %get-tuple-element.78), channel_id=1, source_target_pairs={{0,2},{1,3},{2,0},{3,1},{4,6},{5,7},{6,4},{7,5},{8,10},{9,11},{10,... | collective-permute-start | bytes 983048 | tf_op jit(solution)/shard_map/ppermute | solution.py:726
  5.7 2.1 %collective-permute-start = (s32[2]{0:T(128)S(1)}, s32[2]{0:T(128)S(1)}, u32[]{:S(2)}, u32[]{:S(2)}) collective-permute-start(s32[2]{0:T(128)S(1)} %get-tuple-element.41.mine), channel_id=1, source_target_pairs={{0,4},{2,6},{4,8},{5,1},{6,10},{7,3},{8,12},{9,5},{10,14},{11,7},{... | collective-permute-start | bytes 32 | tf_op jit(solution)/shard_map/ppermute | solution.py:727
  7.8 5.0 %collective-permute-done.2.refs_3_.refs_1_ = bf16[128,1280]{1,0:T(8,128)(2,1)S(1)} collective-permute-done((bf16[128,1280]{1,0:T(8,128)(2,1)S(1)}, bf16[128,1280]{1,0:T(8,128)(2,1)S(1)}, u32[]{:S(2)}, u32[]{:S(2)}) %collective-permute-start.2) | collective-permute-done | bytes 327712 | tf_op jit(solution)/shard_map/ppermute | solution.py:726
  12.8 2.7 %collective-permute-start.4 = (bf16[128,1280]{1,0:T(8,128)(2,1)S(1)}, bf16[128,1280]{1,0:T(8,128)(2,1)S(1)}, u32[]{:S(2)}, u32[]{:S(2)}) collective-permute-start(bf16[128,1280]{1,0:T(8,128)(2,1)S(1)} %collective-permute-done.2.refs_3_.refs_1_), channel_id=1, source_target_pairs={{0,1},{1,0},{2,3},{3,2},{4,5},{5,4},{6,7},{7,6},{8,9},{9,8},{10,11... | collective-permute-start | bytes 983048 | tf_op jit(solution)/shard_map/ppermute | solution.py:35
  15.4 4.4 %collective-permute-done.1.refs_2_.refs_0_ = bf16[128,1280]{1,0:T(8,128)(2,1)S(1)} collective-permute-done((bf16[128,1280]{1,0:T(8,128)(2,1)S(1)}, bf16[128,1280]{1,0:T(8,128)(2,1)S(1)}, u32[]{:S(2)}, u32[]{:S(2)}) %collective-permute-start.1) | collective-permute-done | bytes 327712 | tf_op jit(solution)/shard_map/ppermute | solution.py:726
  19.8 1.5 %collective-permute-start.3 = (bf16[128,1280]{1,0:T(8,128)(2,1)S(1)}, bf16[128,1280]{1,0:T(8,128)(2,1)S(1)}, u32[]{:S(2)}, u32[]{:S(2)}) collective-permute-start(bf16[128,1280]{1,0:T(8,128)(2,1)S(1)} %collective-permute-done.1.refs_2_.refs_0_), channel_id=1, source_target_pairs={{0,1},{1,0},{2,3},{3,2},{4,5},{5,4},{6,7},{7,6},{8,9},{9,8},{10,11... | collective-permute-start | bytes 983048 | tf_op jit(solution)/shard_map/ppermute | solution.py:35
  21.3 3.2 %own_project.2 = (bf16[1024,640]{1,0:T(8,128)(2,1)S(1)}, bf16[512,640]{1,0:T(8,128)(2,1)S(1)}, bf16[512,640]{1,0:T(8,128)(2,1)S(1)}) custom-call(bf16[512,1280]{1,0:T(8,128)(2,1)S(1)} %get-tuple-element.43.x_ref.own, bf16[1280,640]{1,0:T(8,128)(2,1)S(1)} %get-tuple-element.44.refs_0_, bf16[1280,640]{1,0:T(8,128)(2,1)S(1)} %get-tuple-element.45.refs_1_.refs_6_.refs_4_, ...), custom_call_target="tpu_custom_call" | custom-call | flops 2516582400 | bytes 4915200 | tf_op jit(solution)/shard_map/own_project/pallas_call | solution.py:197
  24.6 0.0 copy-start.2
  24.6 0.0 copy-start.3
  24.6 0.0 copy-start.4
  24.6 0.0 collective-permute-done.asked
  24.6 0.6 pick.2
  25.2 3.1 %collective-permute-start.7 = (bf16[128,1280]{1,0:T(8,128)(2,1)S(1)}, bf16[128,1280]{1,0:T(8,128)(2,1)S(1)}, u32[]{:S(2)}, u32[]{:S(2)}) collective-permute-start(bf16[128,1280]{1,0:T(8,128)(2,1)S(1)} %pick.2), channel_id=1, source_target_pairs={{1,5},{3,7},{4,0},{5,9},{6,2},{7,11},{8,4},{9,13},{10,6},{11,15},{... | collective-permute-start | bytes 983048 | tf_op jit(solution)/shard_map/ppermute | solution.py:733
  28.4 2.1 %collective-permute-start.6 = (bf16[128,1280]{1,0:T(8,128)(2,1)S(1)}, bf16[128,1280]{1,0:T(8,128)(2,1)S(1)}, u32[]{:S(2)}, u32[]{:S(2)}) collective-permute-start(bf16[128,1280]{1,0:T(8,128)(2,1)S(1)} %collective-permute-done.2.refs_3_.refs_1_), channel_id=1, source_target_pairs={{0,4},{1,5},{4,8},{5,9},{6,2},{7,3},{8,12},{9,13},{10,6},{11,7},{1... | collective-permute-start | bytes 983048 | tf_op jit(solution)/shard_map/ppermute | solution.py:736
  30.5 3.0 %collective-permute-start.5 = (bf16[128,1280]{1,0:T(8,128)(2,1)S(1)}, bf16[128,1280]{1,0:T(8,128)(2,1)S(1)}, u32[]{:S(2)}, u32[]{:S(2)}) collective-permute-start(bf16[128,1280]{1,0:T(8,128)(2,1)S(1)} %collective-permute-done.1.refs_2_.refs_0_), channel_id=1, source_target_pairs={{0,4},{1,5},{4,8},{5,9},{6,2},{7,3},{8,12},{9,13},{10,6},{11,7},{1... | collective-permute-start | bytes 983048 | tf_op jit(solution)/shard_map/ppermute | solution.py:736
  33.6 0.0 collective-permute-done.4.refs_5_.refs_3_
  33.6 0.0 collective-permute-done.3.refs_4_.refs_2_
  33.6 0.0 copy-done.2
  33.6 0.0 copy-done.3
  33.6 0.0 copy-done.4
  33.6 10.0 %attention.2 = (f32[512,640]{1,0:T(8,128)S(1)}, f32[512,640]{1,0:T(8,128)S(1)}, f32[512,640]{1,0:T(8,128)S(1)}, bf16[128,384]{1,0:T(8,128)(2,1)S(1)}) custom-call(s32[12]{0:T(128)S(1)} %copy-done.3, s32[4,4]{1,0:T(4,128)S(1)} %copy-done.2, s32[4]{0:T(128)S(1)} %copy-done.4, s32[2]{0:T(128)S(1)} %get-tuple-element.41.mine, s32[2]{0:T(128)S(1)} %get-tuple-element.42.yours, ...), custom_call_target="tpu_custom_call" | custom-call | flops 1342177280 | bytes 2621440 | tf_op jit(solution)/shard_map/attention/pallas_call | solution.py:470
  43.6 7.0 %collective-permute-done.7.refs_2_ = bf16[128,1280]{1,0:T(8,128)(2,1)S(1)} collective-permute-done((bf16[128,1280]{1,0:T(8,128)(2,1)S(1)}, bf16[128,1280]{1,0:T(8,128)(2,1)S(1)}, u32[]{:S(2)}, u32[]{:S(2)}) %collective-permute-start.7) | collective-permute-done | bytes 327712 | tf_op jit(solution)/shard_map/ppermute | solution.py:733
  50.6 0.0 collective-permute-done.6.refs_5_.last.refs_1_
  50.6 0.0 collective-permute-done.5.refs_4_.refs_0_
  50.6 0.0 collective-permute-start.8
  50.6 0.5 collective-permute-start.9
  51.1 1.1 %collective-permute-done.8.refs_6_.refs_2_ = bf16[128,1280]{1,0:T(8,128)(2,1)S(1)} collective-permute-done((bf16[128,1280]{1,0:T(8,128)(2,1)S(1)}, bf16[128,1280]{1,0:T(8,128)(2,1)S(1)}, u32[]{:S(2)}, u32[]{:S(2)}) %collective-permute-start.8) | collective-permute-done | bytes 327712 | tf_op jit(solution)/shard_map/ppermute | solution.py:35
  52.2 0.5 collective-permute-done.9.refs_7_.last_s.refs_3_
  52.7 0.6 pick.3
  53.3 4.1 %collective-permute-start.10 = (bf16[128,1280]{1,0:T(8,128)(2,1)S(1)}, bf16[128,1280]{1,0:T(8,128)(2,1)S(1)}, u32[]{:S(2)}, u32[]{:S(2)}) collective-permute-start(bf16[128,1280]{1,0:T(8,128)(2,1)S(1)} %pick.3), channel_id=1, source_target_pairs={{1,5},{3,7},{4,0},{5,9},{6,2},{7,11},{8,4},{9,13},{10,6},{11,15},{... | collective-permute-start | bytes 983048 | tf_op jit(solution)/shard_map/ppermute | solution.py:746
  57.4 0.0 copy-start.5
  57.4 1.5 %own_project.3 = (bf16[512,384]{1,0:T(8,128)(2,1)S(1)}, bf16[512,384]{1,0:T(8,128)(2,1)S(1)}) custom-call(bf16[512,1280]{1,0:T(8,128)(2,1)S(1)} %get-tuple-element.43.x_ref.own, bf16[1280,384]{1,0:T(8,128)(2,1)S(1)} %get-tuple-element.53.refs_8_.refs_0_.wc, bf16[1280,384]{1,0:T(8,128)(2,1)S(1)} %get-tuple-element.59.refs_1_), custom_call_target="tpu_custom_call" | custom-call | flops 1006632960 | bytes 1966080 | tf_op jit(solution)/shard_map/own_project/pallas_call | solution.py:197
  59.0 0.1 collective-permute-start.11
  59.0 0.0 copy-done.5
  59.1 9.6 %shard_map.127.refs_11_ = bf16[512,384]{1,0:T(8,128)(2,1)S(1)} custom-call(s32[12]{0:T(128)S(1)} %copy-done.3, bf16[512,384]{1,0:T(8,128)(2,1)S(1)} %get-tuple-element.60.own_ref, bf16[128,384]{1,0:T(8,128)(2,1)S(1)} %get-tuple-element.61.rim_p, bf16[128,1280]{1,0:T(8,128)(2,1)S(1)} %collective-permute-done.6.refs_5_.last.refs_1_, ...), custom_call_target="tpu_custom_call" | custom-call | flops 1006632960 | bytes 1572864 | tf_op jit(solution)/shard_map/pallas_call | solution.py:676
  68.6 0.0 copy-start
  68.6 0.0 copy-start.1
  68.7 0.0 collective-permute-done.10.refs_4_
  68.7 0.6 collective-permute-start.12
  69.2 2.2 %other_project.1 = (bf16[512,640]{1,0:T(8,128)(2,1)S(1)}, bf16[512,640]{1,0:T(8,128)(2,1)S(1)}) custom-call(bf16[128,1280]{1,0:T(8,128)(2,1)S(1)} %collective-permute-done.5.refs_4_.refs_0_, bf16[128,1280]{1,0:T(8,128)(2,1)S(1)} %collective-permute-done.6.refs_5_.last.refs_1_, bf16[128,1280]{1,0:T(8,128)(2,1)S(1)} %collective-permute-done.8.refs_6_.refs_2_, ...), custom_call_target="tpu_custom_call" | custom-call | flops 1677721600 | bytes 3276800 | tf_op jit(solution)/shard_map/other_project/pallas_call | solution.py:219
  71.4 0.0 collective-permute-done.11.refs_3_
  71.4 0.0 collective-permute-done.12.refs_5_
  71.4 0.0 copy-done
  71.5 0.0 copy-done.1
  71.5 11.6 %attention.3 = (bf16[256,1280]{1,0:T(8,128)(2,1)S(1)}, f32[256,1280]{1,0:T(8,128)S(1)}) custom-call(s32[12]{0:T(128)S(1)} %copy-done.3, s32[4,4]{1,0:T(4,128)S(1)} %copy-done.2, s32[4]{0:T(128)S(1)} %copy-done.4, s32[2]{0:T(128)S(1)} %get-tuple-element.41.mine, s32[2]{0:T(128)S(1)} %get-tuple-element.42.yours, ...), custom_call_target="tpu_custom_call" | custom-call | flops 1342177280 | bytes 2621440 | tf_op jit(solution)/shard_map/attention/pallas_call | solution.py:470
  83.0 0.1 collective-permute-start.13
  83.1 2.1 %collective-permute-done.13 = bf16[256,1280]{1,0:T(8,128)(2,1)S(1)} collective-permute-done((bf16[256,1280]{1,0:T(8,128)(2,1)S(1)}, bf16[256,1280]{1,0:T(8,128)(2,1)S(1)}, u32[]{:S(2)}, u32[]{:S(2)}) %collective-permute-start.13) | collective-permute-done | bytes 655392 | tf_op jit(solution)/shard_map/ppermute | solution.py:35
  85.2 1.0 %add_convert_fusion = bf16[256,1280]{1,0:T(8,128)(2,1)} fusion(f32[256,1280]{1,0:T(8,128)S(1)} %get-tuple-element.75, bf16[256,1280]{1,0:T(8,128)(2,1)S(1)} %collective-permute-done.13), kind=kLoop, calls=%fused_computation | loop fusion | flops 983040 | bytes 2621440 | tf_op jit(solution)/shard_map/convert_element_type | solution.py:762
  (1 shorter events, 0.0 us)
Async XLA Ops:
  4.1 8.7 %collective-permute-start.2 = (bf16[128,1280]{1,0:T(8,128)(2,1)S(1)}, bf16[128,1280]{1,0:T(8,128)(2,1)S(1)}, u32[]{:S(2)}, u32[]{:S(2)}) collective-permute-start(bf16[128,1280]{1,0:T(8,128)(2,1)S(1)} %get-tuple-element.77), channel_id=1, source_target_pairs={{0,2},{1,3},{2,0},{3,1},{4,6},{5,7},{6,4},{7,5},{8,10},{9,11},{10,... | collective-permute-start | bytes 983048 | tf_op jit(solution)/shard_map/ppermute | solution.py:726
  4.4 15.4 %collective-permute-start.1 = (bf16[128,1280]{1,0:T(8,128)(2,1)S(1)}, bf16[128,1280]{1,0:T(8,128)(2,1)S(1)}, u32[]{:S(2)}, u32[]{:S(2)}) collective-permute-start(bf16[128,1280]{1,0:T(8,128)(2,1)S(1)} %get-tuple-element.78), channel_id=1, source_target_pairs={{0,2},{1,3},{2,0},{3,1},{4,6},{5,7},{6,4},{7,5},{8,10},{9,11},{10,... | collective-permute-start | bytes 983048 | tf_op jit(solution)/shard_map/ppermute | solution.py:726
  5.7 19.0 %collective-permute-start = (s32[2]{0:T(128)S(1)}, s32[2]{0:T(128)S(1)}, u32[]{:S(2)}, u32[]{:S(2)}) collective-permute-start(s32[2]{0:T(128)S(1)} %get-tuple-element.41.mine), channel_id=1, source_target_pairs={{0,4},{2,6},{4,8},{5,1},{6,10},{7,3},{8,12},{9,5},{10,14},{11,7},{... | collective-permute-start | bytes 32 | tf_op jit(solution)/shard_map/ppermute | solution.py:727
  12.8 20.8 %collective-permute-start.4 = (bf16[128,1280]{1,0:T(8,128)(2,1)S(1)}, bf16[128,1280]{1,0:T(8,128)(2,1)S(1)}, u32[]{:S(2)}, u32[]{:S(2)}) collective-permute-start(bf16[128,1280]{1,0:T(8,128)(2,1)S(1)} %collective-permute-done.2.refs_3_.refs_1_), channel_id=1, source_target_pairs={{0,1},{1,0},{2,3},{3,2},{4,5},{5,4},{6,7},{7,6},{8,9},{9,8},{10,11... | collective-permute-start | bytes 983048 | tf_op jit(solution)/shard_map/ppermute | solution.py:35
  19.8 13.8 %collective-permute-start.3 = (bf16[128,1280]{1,0:T(8,128)(2,1)S(1)}, bf16[128,1280]{1,0:T(8,128)(2,1)S(1)}, u32[]{:S(2)}, u32[]{:S(2)}) collective-permute-start(bf16[128,1280]{1,0:T(8,128)(2,1)S(1)} %collective-permute-done.1.refs_2_.refs_0_), channel_id=1, source_target_pairs={{0,1},{1,0},{2,3},{3,2},{4,5},{5,4},{6,7},{7,6},{8,9},{9,8},{10,11... | collective-permute-start | bytes 983048 | tf_op jit(solution)/shard_map/ppermute | solution.py:35
  24.6 9.0 %copy-start.2 = (s32[4,4]{1,0:T(4,128)S(1)}, s32[4,4]{1,0:T(4,128)}, u32[]{:S(2)}) copy-start(s32[4,4]{1,0:T(4,128)} %lists.3) | copy-start | bytes 196
  24.6 9.0 %copy-start.3 = (s32[12]{0:T(128)S(1)}, s32[12]{0:T(128)}, u32[]{:S(2)}) copy-start(s32[12]{0:T(128)} %starts.5) | copy-start | bytes 148
  24.6 9.0 %copy-start.4 = (s32[4]{0:T(128)S(1)}, s32[4]{0:T(128)}, u32[]{:S(2)}) copy-start(s32[4]{0:T(128)} %counts.3) | copy-start | bytes 52
  25.2 25.4 %collective-permute-start.7 = (bf16[128,1280]{1,0:T(8,128)(2,1)S(1)}, bf16[128,1280]{1,0:T(8,128)(2,1)S(1)}, u32[]{:S(2)}, u32[]{:S(2)}) collective-permute-start(bf16[128,1280]{1,0:T(8,128)(2,1)S(1)} %pick.2), channel_id=1, source_target_pairs={{1,5},{3,7},{4,0},{5,9},{6,2},{7,11},{8,4},{9,13},{10,6},{11,15},{... | collective-permute-start | bytes 983048 | tf_op jit(solution)/shard_map/ppermute | solution.py:733
  28.4 22.2 %collective-permute-start.6 = (bf16[128,1280]{1,0:T(8,128)(2,1)S(1)}, bf16[128,1280]{1,0:T(8,128)(2,1)S(1)}, u32[]{:S(2)}, u32[]{:S(2)}) collective-permute-start(bf16[128,1280]{1,0:T(8,128)(2,1)S(1)} %collective-permute-done.2.refs_3_.refs_1_), channel_id=1, source_target_pairs={{0,4},{1,5},{4,8},{5,9},{6,2},{7,3},{8,12},{9,13},{10,6},{11,7},{1... | collective-permute-start | bytes 983048 | tf_op jit(solution)/shard_map/ppermute | solution.py:736
  30.5 20.1 %collective-permute-start.5 = (bf16[128,1280]{1,0:T(8,128)(2,1)S(1)}, bf16[128,1280]{1,0:T(8,128)(2,1)S(1)}, u32[]{:S(2)}, u32[]{:S(2)}) collective-permute-start(bf16[128,1280]{1,0:T(8,128)(2,1)S(1)} %collective-permute-done.1.refs_2_.refs_0_), channel_id=1, source_target_pairs={{0,4},{1,5},{4,8},{5,9},{6,2},{7,3},{8,12},{9,13},{10,6},{11,7},{1... | collective-permute-start | bytes 983048 | tf_op jit(solution)/shard_map/ppermute | solution.py:736
  50.6 1.6 %collective-permute-start.8 = (bf16[128,1280]{1,0:T(8,128)(2,1)S(1)}, bf16[128,1280]{1,0:T(8,128)(2,1)S(1)}, u32[]{:S(2)}, u32[]{:S(2)}) collective-permute-start(bf16[128,1280]{1,0:T(8,128)(2,1)S(1)} %collective-permute-done.5.refs_4_.refs_0_), channel_id=1, source_target_pairs={{0,1},{1,0},{2,3},{3,2},{4,5},{5,4},{6,7},{7,6},{8,9},{9,8},{10,11... | collective-permute-start | bytes 983048 | tf_op jit(solution)/shard_map/ppermute | solution.py:35
  50.6 2.1 %collective-permute-start.9 = (bf16[128,1280]{1,0:T(8,128)(2,1)S(1)}, bf16[128,1280]{1,0:T(8,128)(2,1)S(1)}, u32[]{:S(2)}, u32[]{:S(2)}) collective-permute-start(bf16[128,1280]{1,0:T(8,128)(2,1)S(1)} %collective-permute-done.6.refs_5_.last.refs_1_), channel_id=1, source_target_pairs={{0,1},{1,0},{2,3},{3,2},{4,5},{5,4},{6,7},{7,6},{8,9},{9,8},{10,11... | collective-permute-start | bytes 983048 | tf_op jit(solution)/shard_map/ppermute | solution.py:35
  53.3 15.3 %collective-permute-start.10 = (bf16[128,1280]{1,0:T(8,128)(2,1)S(1)}, bf16[128,1280]{1,0:T(8,128)(2,1)S(1)}, u32[]{:S(2)}, u32[]{:S(2)}) collective-permute-start(bf16[128,1280]{1,0:T(8,128)(2,1)S(1)} %pick.3), channel_id=1, source_target_pairs={{1,5},{3,7},{4,0},{5,9},{6,2},{7,11},{8,4},{9,13},{10,6},{11,15},{... | collective-permute-start | bytes 983048 | tf_op jit(solution)/shard_map/ppermute | solution.py:746
  57.4 1.6 %copy-start.5 = (bf16[128,384]{1,0:T(8,128)(2,1)S(1)}, bf16[128,384]{1,0:T(8,128)(2,1)}, u32[]{:S(2)}) copy-start(bf16[128,384]{1,0:T(8,128)(2,1)} %taps_ref.1) | copy-start | bytes 294916
  59.0 12.5 %collective-permute-start.11 = (bf16[128,1280]{1,0:T(8,128)(2,1)S(1)}, bf16[128,1280]{1,0:T(8,128)(2,1)S(1)}, u32[]{:S(2)}, u32[]{:S(2)}) collective-permute-start(bf16[128,1280]{1,0:T(8,128)(2,1)S(1)} %collective-permute-done.7.refs_2_), channel_id=1, source_target_pairs={{0,1},{1,0},{2,3},{3,2},{4,5},{5,4},{6,7},{7,6},{8,9},{9,8},{10,11... | collective-permute-start | bytes 983048 | tf_op jit(solution)/shard_map/ppermute | solution.py:35
  68.6 2.8 %copy-start = (bf16[640,1280]{1,0:T(8,128)(2,1)S(1)}, bf16[640,1280]{1,0:T(8,128)(2,1)}, u32[]{:S(2)}) copy-start(bf16[640,1280]{1,0:T(8,128)(2,1)} %refs_12_.1) | copy-start | bytes 4915204
  68.6 2.8 %copy-start.1 = (bf16[384,1280]{1,0:T(8,128)(2,1)S(1)}, bf16[384,1280]{1,0:T(8,128)(2,1)}, u32[]{:S(2)}) copy-start(bf16[384,1280]{1,0:T(8,128)(2,1)} %refs_13_.1) | copy-start | bytes 2949124
  68.7 2.8 %collective-permute-start.12 = (bf16[128,1280]{1,0:T(8,128)(2,1)S(1)}, bf16[128,1280]{1,0:T(8,128)(2,1)S(1)}, u32[]{:S(2)}, u32[]{:S(2)}) collective-permute-start(bf16[128,1280]{1,0:T(8,128)(2,1)S(1)} %collective-permute-done.10.refs_4_), channel_id=1, source_target_pairs={{0,1},{1,0},{2,3},{3,2},{4,5},{5,4},{6,7},{7,6},{8,9},{9,8},{10,11... | collective-permute-start | bytes 983048 | tf_op jit(solution)/shard_map/ppermute | solution.py:35
  83.0 2.2 %collective-permute-start.13 = (bf16[256,1280]{1,0:T(8,128)(2,1)S(1)}, bf16[256,1280]{1,0:T(8,128)(2,1)S(1)}, u32[]{:S(2)}, u32[]{:S(2)}) collective-permute-start(bf16[256,1280]{1,0:T(8,128)(2,1)S(1)} %get-tuple-element.76), channel_id=1, source_target_pairs={{0,1},{1,0},{2,3},{3,2},{4,5},{5,4},{6,7},{7,6},{8,9},{9,8},{10,11... | collective-permute-start | bytes 1966088 | tf_op jit(solution)/shard_map/ppermute | solution.py:35

commit v2 on v1

--- a/solution.py
+++ b/solution.py
@@ -58,22 +58,30 @@
 def plan_kernel(per_shard, nweights, lists_in, tokens, gain_in, *refs):
     weights, refs = refs[:nweights], refs[nweights:]
     mine, yours, normed, half, *refs = refs
-    kept, (lists, gain, rows, sem) = refs[:nweights], refs[nweights:]
+    every, lists, gain, rows, sem = refs
+    kept, column = [], 0
+    for w in weights:
+        kept.append(every.at[:, pl.ds(column, w.shape[1])])
+        column += w.shape[1]
     me, core = lax.axis_index("seq"), lax.axis_index("head")
     size = tokens.shape[0] // PIECES
+    small = [
+        pltpu.make_async_copy(lists_in, lists, sem.at[PIECES]),
+        pltpu.make_async_copy(gain_in, gain, sem.at[PIECES + 1]),
+    ]
     copies = [
         pltpu.make_async_copy(
             tokens.at[pl.ds(n * size, size)], rows.at[pl.ds(n * size, size)], sem.at[n]
         )
         for n in range(PIECES)
     ]
-    copies.append(pltpu.make_async_copy(lists_in, lists, sem.at[PIECES]))
-    copies.append(pltpu.make_async_copy(gain_in, gain, sem.at[PIECES + 1]))
-    for n in range(nweights):
-        copies.append(pltpu.make_async_copy(weights[n], kept[n], sem.at[PIECES + 2 + n]))
-    for copy in copies:
+    copies += [
+        pltpu.make_async_copy(weights[n], kept[n], sem.at[PIECES + 2 + n]) for n in range(nweights)
+    ]
+    for copy in small + copies:
         copy.start()
-    copies[PIECES + 1].wait()
+    for copy in small:
+        copy.wait()
     g = jnp.broadcast_to(gain[...].reshape(1, -1), (32, normed.shape[1]))
 
     def norm(r, c):
@@ -86,7 +94,6 @@
     for n in range(PIECES):
         copies[n].wait()
         lax.fori_loop(n * size // 32, (n + 1) * size // 32, norm, 0)
-    copies[PIECES].wait()
 
     def wanted(distance):
         low = (me + distance) * per_shard
@@ -103,7 +110,7 @@
         yours[n] = wanted(-side * (n + 2))
     count = half.shape[0]
     half[...] = normed[pl.ds(pl.multiple_of(core * count, count), count), :]
-    for copy in copies[PIECES + 2 :]:
+    for copy in copies[PIECES:]:
         copy.wait()
 
 
@@ -118,9 +125,9 @@
             jax.ShapeDtypeStruct((rows, cols), BF16),
             jax.ShapeDtypeStruct((rows // 2, cols), BF16),
         ]
-        + [jax.ShapeDtypeStruct(w.shape, BF16) for w in weights],
+        + [jax.ShapeDtypeStruct((cols, sum(w.shape[1] for w in weights)), BF16)],
         in_specs=[ANY] * (3 + len(weights)),
-        out_specs=[SMEM, SMEM] + [VMEM] * (2 + len(weights)),
+        out_specs=[SMEM, SMEM] + [VMEM] * 3,
         scratch_shapes=[
             pltpu.SMEM(lists.shape, jnp.int32),
             pltpu.VMEM(gain.shape, F32),
@@ -173,60 +180,81 @@
     return jnp.where(lax.axis_index("head") == 1, mine[last, :], swapped[last, :])
 
 
-def own_kernel(scale, x_ref, *refs):
-    count = len(refs) // 2
-    weights, outs = refs[:count], refs[count:]
-    rows = x_ref.shape[0]
-    for n in range(count):
-        y = dot(x_ref[...], weights[n][...])
-        if n == 0 and scale is not None:
+WIDE = 2 * LANES
+
+
+def products(x, weights, columns, outs):
+    where = []
+    for width, store in outs:
+        where += [(store, c) for c in range(0, width, LANES)]
+    total = len(where) * LANES
+    for n in range(0, total, WIDE):
+        last = min(n + WIDE, total)
+        y = dot(x, weights[:, columns + n : columns + last])
+        for c in range(n, last, LANES):
+            store, column = where[c // LANES]
+            store(slice(column, column + LANES), y[:, c - n : c - n + LANES])
+
+
+def stored_in(ref, rows=slice(None)):
+    def store(cols, y):
+        ref[rows, cols] = y.astype(BF16)
+
+    return ref.shape[1], store
+
+
+def own_kernel(columns, scale, x_ref, weights, *outs):
+    targets = [stored_in(out) for out in outs]
+    if scale is not None:
+        q_ref, rows = outs[0], x_ref.shape[0]
+        low = lax.broadcasted_iota(jnp.int32, (rows, LANES), 1) < HD
+
+        def store(cols, y):
             y = (y * scale).astype(BF16)
-            low = lax.broadcasted_iota(jnp.int32, y.shape, 1) % LANES < HD
-            outs[n][:rows, :] = jnp.where(low, y, jnp.zeros_like(y))
-            outs[n][rows:, :] = jnp.where(low, jnp.zeros_like(y), y)
-        else:
-            outs[n][...] = y.astype(BF16)
-
-
-def own_project(x, weights, scale=None):
+            q_ref[:rows, cols] = jnp.where(low, y, jnp.zeros_like(y))
+            q_ref[rows:, cols] = jnp.where(low, jnp.zeros_like(y), y)
+
+        targets[0] = (q_ref.shape[1], store)
+    products(x_ref[...], weights, columns, targets)
+
+
+def own_project(x, weights, columns, widths, scale=None):
     rows, cols = x.shape
-    outs = [jax.ShapeDtypeStruct((rows, w.shape[1]), BF16) for w in weights]
+    outs = [jax.ShapeDtypeStruct((rows, width), BF16) for width in widths]
     if scale is not None:
-        outs[0] = jax.ShapeDtypeStruct((2 * rows, weights[0].shape[1]), BF16)
-    flops = sum(2 * rows * cols * w.shape[1] for w in weights)
+        outs[0] = jax.ShapeDtypeStruct((2 * rows, widths[0]), BF16)
     return pl.pallas_call(
-        functools.partial(own_kernel, scale),
+        functools.partial(own_kernel, columns, scale),
         out_shape=outs,
-        in_specs=[VMEM] * (1 + len(weights)),
+        in_specs=[VMEM] * 2,
         out_specs=[VMEM] * len(outs),
+        compiler_params=limit(16),
+        cost_estimate=pl.CostEstimate(
+            flops=2 * rows * cols * sum(widths), bytes_accessed=2 * cols * sum(widths), transcendentals=0
+        ),
+        name="own_project",
+    )(x, weights)
+
+
+def other_kernel(columns, *refs):
+    *parts, weights, k_ref, v_ref = refs
+    x = jnp.concatenate([part[...] for part in parts], axis=0)
+    products(x, weights, columns, [stored_in(k_ref), stored_in(v_ref)])
+
+
+def other_project(parts, weights, columns, width):
+    rows, cols = sum(part.shape[0] for part in parts), parts[0].shape[1]
+    return pl.pallas_call(
+        functools.partial(other_kernel, columns),
+        out_shape=[jax.ShapeDtypeStruct((rows, width), BF16)] * 2,
+        in_specs=[VMEM] * (1 + len(parts)),
+        out_specs=[VMEM] * 2,
         compiler_params=limit(14),
         cost_estimate=pl.CostEstimate(
-            flops=flops, bytes_accessed=sum(w.size * 2 for w in weights), transcendentals=0
-        ),
-        name="own_project",
-    )(x, *weights)
-
-
-def other_kernel(*refs):
-    *parts, wk, wv, k_ref, v_ref = refs
-    x = jnp.concatenate([part[...] for part in parts], axis=0)
-    k_ref[...] = dot(x, wk[...]).astype(BF16)
-    v_ref[...] = dot(x, wv[...]).astype(BF16)
-
-
-def other_project(parts, wk, wv):
-    rows, cols = sum(part.shape[0] for part in parts), parts[0].shape[1]
-    return pl.pallas_call(
-        other_kernel,
-        out_shape=[jax.ShapeDtypeStruct((rows, w.shape[1]), BF16) for w in (wk, wv)],
-        in_specs=[VMEM] * (2 + len(parts)),
-        out_specs=[VMEM] * 2,
-        compiler_params=limit(10),
-        cost_estimate=pl.CostEstimate(
-            flops=4 * rows * cols * wk.shape[1], bytes_accessed=4 * wk.size, transcendentals=0
+            flops=4 * rows * cols * width, bytes_accessed=4 * cols * width, transcendentals=0
         ),
         name="other_project",
-    )(*parts, wk, wv)
+    )(*parts, weights)
 
 
 BIG = 1 << 30
@@ -234,7 +262,8 @@
 
 
 def attention_kernel(
-    first,
+    stage,
+    columns,
     fresh_parts,
     nch,
     per_shard,
@@ -245,25 +274,32 @@
     mine,
     yours,
     q_ref,
+    k_in,
+    v_in,
     *refs,
 ):
-    k_in, v_in, *refs = refs
-    new, (wk, wv, *refs) = refs[:fresh_parts], refs[fresh_parts:]
+    first = stage == 0
+    new, refs = refs[:fresh_parts], refs[fresh_parts:]
+    if stage < 2:
+        weights, *refs = refs
     if first:
-        wc_in, o_ref, l_ref, mx_ref, rim_ref, *refs = refs
+        o_ref, l_ref, mx_ref, rim_ref, k_all, v_all, *refs = refs
     else:
-        o_ref, l_ref, mx_ref, g_ref, wo, wco, theirs, ours, *refs = refs
-    k_all, v_all, s_buf, m_buf, bias, k_chain, i_chain, gblk, flag, ids, around, *refs = refs
+        o_ref, l_ref, mx_ref, g_ref, wo, wco, out_ref, *refs = refs
+        k_all, v_all, refs = (refs[0], refs[1], refs[2:]) if stage == 1 else (k_in, v_in, refs)
+    s_buf, m_buf, bias, k_chain, i_chain, gblk, flag, ids, around, *refs = refs
     a_ref = None if first else refs[0]
     pairs = q_ref.shape[1] // LANES
-    held = k_in.shape[0]
-    k_all[:held] = k_in[...]
-    v_all[:held] = v_in[...]
-    fresh = jnp.concatenate([part[...] for part in new], axis=0)
-    k_all[held:] = dot(fresh, wk[...]).astype(BF16)
-    v_all[held:] = dot(fresh, wv[...]).astype(BF16)
+    if stage < 2:
+        held = k_in.shape[0]
+        k_all[:held] = k_in[...]
+        v_all[:held] = v_in[...]
+        fresh = jnp.concatenate([part[...] for part in new], axis=0)
+        rest = slice(held, None)
+        products(fresh, weights, columns, [stored_in(k_all, rest), stored_in(v_all, rest)])
     if first:
-        rim_ref[...] = dot(rim_rows(new), wc_in[...]).astype(BF16)
+        conv_columns = columns + 2 * k_in.shape[1]
+        products(rim_rows(new), weights, conv_columns, [stored_in(rim_ref)])
 
     me, core = lax.axis_index("seq"), lax.axis_index("head")
     shards = lax.axis_size("seq")
@@ -332,7 +368,11 @@
     for n, value in enumerate(lax.fori_loop(0, nch, scan, none * per_shard)):
         around[n] = value
 
-    def one_block(qb, carry):
+    blocks = per_shard if first else per_shard // 2
+    q_base = (0, (1 - core) * blocks, core * blocks)[stage]
+
+    def one_block(t, carry):
+        qb = q_base + t
         gq = own + qb
         q_first = gq * BLK
         q_last = q_first + BLK - 1
@@ -425,7 +465,8 @@
                     scale = jnp.exp2(mx_ref[q_rows, cols] - m)
                     o = o + o_ref[q_rows, cols] * scale
                     l = l + l_ref[q_rows, cols] * scale
-                    a_ref[q_rows, cols] = (o / l).astype(BF16)
+                    a_rows = pl.ds(pl.multiple_of(t * BLK, BLK), BLK)
+                    a_ref[a_rows, cols] = (o / l).astype(BF16)
 
             scores(0)
             for p in range(pairs):
@@ -441,40 +482,41 @@
 
         return carry
 
-    lax.fori_loop(0, per_shard, one_block, 0)
+    lax.fori_loop(0, blocks, one_block, 0)
     if not first:
-        rows = ours.shape[0]
-        for half, out in ((1 - core, theirs), (core, ours)):
-            here = pl.ds(pl.multiple_of(half * rows, rows), rows)
-            y = dot(a_ref[here, :], wo[...]) + dot(g_ref[here, :], wco[...])
-            out[...] = y.astype(out.dtype)
-
-
-def attention(context, queries, kv, new, weights, finish=None):
-    rows, cols = kv[0].shape
+        here = pl.ds(pl.multiple_of(q_base * BLK, BLK), blocks * BLK)
+        y = dot(a_ref[...], wo[...]) + dot(g_ref[here, :], wco[...])
+        out_ref[...] = y.astype(out_ref.dtype)
+
+
+def attention(stage, context, queries, kv, new=(), weights=(), finish=(), columns=0, rim=0):
+    rows, cols = queries.shape[0] // 2, queries.shape[1]
     pairs = cols // LANES
-    fresh = sum(part.shape[0] for part in new)
-    keys = kv[0].shape[0] + fresh
+    keys = kv[0].shape[0] + sum(part.shape[0] for part in new)
     kblocks = keys // BLK
     steps = (kblocks + 1) // 2
-    first = finish is None
-    sums = jax.ShapeDtypeStruct((rows, cols), F32)
-    if first:
-        extra, more = (), []
-        out_shape = [sums] * 3 + [jax.ShapeDtypeStruct((KTAP, weights[2].shape[1]), BF16)]
+    held = jax.ShapeDtypeStruct((keys, cols), BF16)
+    more = []
+    if stage == 0:
+        out_shape = [jax.ShapeDtypeStruct((rows, cols), F32)] * 3
+        out_shape += [jax.ShapeDtypeStruct((KTAP, rim), BF16)]
+        kept = [pltpu.VMEM(held.shape, BF16)] * 2
     else:
-        extra, more = finish, [pltpu.VMEM((rows, cols), BF16)]
+        kept, more = [], [pltpu.VMEM((rows // 2, cols), BF16)]
         wide = finish[4].shape[1]
-        out_shape = [jax.ShapeDtypeStruct((rows // 2, wide), t) for t in (BF16, F32)]
-    operands = (queries, *kv, *new, *weights, *extra)
+        out_shape = [jax.ShapeDtypeStruct((rows // 2, wide), BF16 if stage == 1 else F32)]
+        if stage == 1:
+            out_shape += [held] * 2
+    operands = (queries, *kv, *new, *weights, *finish)
+    here = rows if stage == 0 else rows // 2
     return pl.pallas_call(
         functools.partial(
-            attention_kernel, first, len(new), context[0].shape[0], rows // BLK, kblocks
+            attention_kernel, stage, columns, len(new), context[0].shape[0], rows // BLK, kblocks
         ),
         out_shape=out_shape,
         in_specs=[SMEM] * len(context) + [VMEM] * len(operands),
         out_specs=[VMEM] * len(out_shape),
-        scratch_shapes=[pltpu.VMEM((keys, cols), BF16)] * 2
+        scratch_shapes=kept
         + [
             pltpu.VMEM((pairs, steps, 2 * BLK, 2 * BLK), F32),
             pltpu.VMEM((pairs, 2 * BLK, LANES), F32),
@@ -487,9 +529,9 @@
             pltpu.SMEM((4 * rows // BLK,), jnp.int32),
         ]
         + more,
-        compiler_params=limit(32),
+        compiler_params=limit(20),
         cost_estimate=pl.CostEstimate(
-            flops=4 * rows * keys * cols, bytes_accessed=4 * keys * cols, transcendentals=rows * keys
+            flops=4 * here * keys * cols, bytes_accessed=4 * keys * cols, transcendentals=here * keys
         ),
         name="attention",
     )(*context, *operands)
@@ -508,7 +550,7 @@
 
 
 def conv_kernel(
-    nch, starts, own_ref, rim_p, last, last_s, wc, taps_ref, gate_ref, out_ref, x_ref, xs, ws, ms, y, xl, tf, y2
+    nch, columns, starts, own_ref, rim_p, last, last_s, weights, taps_ref, gate_ref, out_ref, x_ref, xs, ws, ms, y, xl, tf, y2
 ):
     rows, cols = own_ref.shape
     span = rows // SEG
@@ -529,7 +571,8 @@
     inner = begin > 0
     outer_begin = jnp.where(inner, -(1 << 30), begin)
 
-    rim_o = dot(rim_rows((last, last_s)), wc[...]).astype(BF16)
+    wc = weights[:, columns : columns + cols]
+    rim_o = dot(rim_rows((last, last_s)), wc).astype(BF16)
     for t in range(tiles):
         cols_t = slice(t * LANES, (t + 1) * LANES)
         x_ref[t, 0:KTAP, :] = jnp.where(me % 2 == 1, rim_p[:, cols_t], rim_o[:, cols_t]).astype(F32)
@@ -562,7 +605,7 @@
         quarter + outs,
         spread,
         tuple(row_of(start + k, t) for t in range(tiles) for k in (-3, -2, -1)),
-        unroll=2,
+        unroll=4,
     )
 
     def widen(g, c):
@@ -606,7 +649,7 @@
                 y[4 * b + 2 * k, :, cols_t] = m1 - m2
             return c
 
-        lax.fori_loop(0, outs, join, 0)
+        lax.fori_loop(0, outs, join, 0, unroll=4)
 
     def collect(j, c):
         for t in range(tiles):
@@ -668,13 +711,13 @@
     lax.fori_loop(0, rows // 64, gating, 0)
 
 
-def convolution(starts, own, rim_p, last, last_s, wc, taps, gate):
+def convolution(columns, starts, own, rim_p, last, last_s, weights, taps, gate):
     rows, cols = own.shape
     span = rows // SEG
     quarter, outs = KTAP // 4, span // 4
     tiles = cols // LANES
     return pl.pallas_call(
-        functools.partial(conv_kernel, starts.shape[0]),
+        functools.partial(conv_kernel, starts.shape[0], columns),
         out_shape=jax.ShapeDtypeStruct((rows, cols), BF16),
         in_specs=[SMEM] + [VMEM] * 7,
         out_specs=VMEM,
@@ -692,7 +735,7 @@
         cost_estimate=pl.CostEstimate(
             flops=40 * rows * cols * KTAP, bytes_accessed=8 * rows * cols, transcendentals=rows * cols
         ),
-    )(starts, own, rim_p, last, last_s, wc, taps, gate)
+    )(starts, own, rim_p, last, last_s, weights, taps, gate)
 
 
 def body(
@@ -713,7 +756,9 @@
     shards = lax.axis_size("seq")
 
     after = lax.optimization_barrier
-    mine, yours, normed, half, w_query, w_key, w_value, conv_in_w, conv_gate_w = plan(
+    head_cols, channels = w_query.shape[1], conv_in_w.shape[1]
+    kv_columns, conv_columns = head_cols, 3 * head_cols
+    mine, yours, normed, half, weights = plan(
         block_lists, tokens, norm_gain, (w_query, w_key, w_value, conv_in_w, conv_gate_w)
     )
     to_asking = flat_pairs(shards, lambda i, h: i + (-2 if h == 0 else 2))
@@ -727,39 +772,59 @@
     asked = lax.ppermute(mine, AXES, to_asked)
 
     scale = math.log2(math.e) / math.sqrt(HD)
-    queries, k_own, v_own = own_project(normed, (w_query, w_key, w_value), scale)
+    queries, k_own, v_own = own_project(normed, weights, 0, (head_cols,) * 3, scale)
     asked, k_own = after((asked, k_own))
     picked = pick(asked, (normed,))
     far = lax.ppermute(picked, AXES, to_asking)
-    conv_input, conv_gate = own_project(normed, (conv_in_w, conv_gate_w))
+    conv_input, conv_gate = own_project(normed, weights, conv_columns, (channels,) * 2)
     for n in range(2):
         other[n] = lax.ppermute(partner[n], AXES, to_other)
     partner += [swap(part) for part in partner]
 
     context = (chain_starts, block_lists, block_counts, mine, yours)
     *state, rim_p = attention(
-        context, queries, (k_own, v_own), partner, (w_key, w_value, conv_in_w)
+        0,
+        context,
+        queries,
+        (k_own, v_own),
+        partner,
+        (weights,),
+        columns=kv_columns,
+        rim=channels,
     )
-    other, far, state = after((other, far, state))
+    other, state = after((other, state))
     other += [swap(part) for part in other]
+    farther = lax.ppermute(pick(asked, (*partner, *other)), AXES, to_asking)
+
+    gated = convolution(
+        conv_columns,
+        chain_starts,
+        conv_input,
+        rim_p,
+        other[1],
+        other[3],
+        weights,
+        conv_taps,
+        conv_gate,
+    )
+    far, farther, gated, other = after((far, farther, gated, other))
     far_s = swap(far)
-    farther = lax.ppermute(pick(asked, (*partner, *other)), AXES, to_asking)
-
-    gated = convolution(
-        chain_starts, conv_input, rim_p, other[1], other[3], conv_in_w, conv_taps, conv_gate
-    )
-    farther, gated, other = after((farther, gated, other))
     farther_s = swap(farther)
-    k_o, v_o = other_project(other, w_key, w_value)
-    theirs, ours = attention(
+    k_o, v_o = other_project(other, weights, kv_columns, head_cols)
+    finish = (*state, gated, w_out, conv_out_w)
+    theirs, k_rest, v_rest = attention(
+        1,
         context,
         queries,
         (k_o, v_o),
         (far, far_s, farther, farther_s),
-        (w_key, w_value),
-        (*state, gated, w_out, conv_out_w),
+        (weights,),
+        finish,
+        kv_columns,
     )
-    return (ours + swap(theirs).astype(F32)).astype(BF16)
+    theirs = swap(theirs)
+    (ours,) = attention(2, context, queries, (k_rest, v_rest), finish=finish)
+    return (ours + theirs.astype(F32)).astype(BF16)
 
 
 def solution(mesh):

time: 86.9 us -> 82.5 us (0.949)
  the two profiles are of different devices: /device:TPU:15 before, /device:TPU:16 now
where the time goes in v2:
time: 82.5 us; the launch traced here: 82.2 us
  Pallas kernels  43.3 us (52%)
  starting transfers between devices  20.9 us (25%)
  waiting for transfers between devices  16.7 us (20%)
  other arithmetic  0.99 us (1%)
    pallas_call x3, Pallas kernels, attention(): pl.pallas_call(functools.partial(attention_kernel, stage, columns, len(ne...  23.1 us
    ppermute x2, waiting for transfers between devices, body(): partner[n] = lax.ppermute(chunks[n], AXES, to_partner)  14.4 us
    pallas_call x1, Pallas kernels, convolution(): pl.pallas_call(functools.partial(conv_kernel, starts.shape[0], columns),...  8.89 us
    ppermute x2, starting transfers between devices, body(): other[n] = lax.ppermute(partner[n], AXES, to_other)  6.86 us
    ppermute x1, starting transfers between devices, body(): far = lax.ppermute(picked, AXES, to_asking)  4.25 us
    pallas_call x2, Pallas kernels, own_project(): pl.pallas_call(functools.partial(own_kernel, columns, scale), out_shape=o...  4.15 us
    pallas_call x1, Pallas kernels, plan(): pl.pallas_call(functools.partial(plan_kernel, rows // BLK, len(weights)),...  4.06 us
    ppermute x1, starting transfers between devices, body(): asked = lax.ppermute(mine, AXES, to_asked)  3.42 us
  transfers between devices with their start and end apart: 14, of which 3 were waited for; matrix products, arithmetic and copies ran while one was open for 0% of the time, Pallas kernels for 39%

profile of v2, /device:TPU:16, one launch (start us, length us, event | category | flops | bytes accessed | tf_op | source)
XLA Modules:
  0.0 82.2 jit_solution(4659887568554060086)
XLA Ops:
  0.0 4.1 %plan.1 = (s32[2]{0:T(128)S(1)}, s32[2]{0:T(128)S(1)}, bf16[512,1280]{1,0:T(8,128)(2,1)S(1)}, bf16[256,1280]{1,0:T(8,128)(2,1)S(1)}, bf16[1280,2688]{1,0:T(8,128)(2,1)S(1)}) custom-call(s32[4,4]{1,0:T(4,128)} %lists.5, bf16[512,1280]{1,0:T(8,128)(2,1)} %tokens.1, f32[1280]{0:T(1024)} %gain_in.1, bf16[1280,640]{1,0:T(8,128)(2,1)} %refs_0_.1, ...), custom_call_target="tpu_custom_call" | custom-call | tf_op jit(solution)/shard_map/plan/pallas_call | solution.py:120
  4.1 1.6 %collective-permute-start.3 = (bf16[128,1280]{1,0:T(8,128)(2,1)S(1)}, bf16[128,1280]{1,0:T(8,128)(2,1)S(1)}, u32[]{:S(2)}, u32[]{:S(2)}) collective-permute-start(bf16[128,1280]{1,0:T(8,128)(2,1)S(1)} %get-tuple-element.71), channel_id=1, source_target_pairs={{0,2},{1,3},{2,0},{3,1},{4,6},{5,7},{6,4},{7,5},{8,10},{9,11},{10,... | collective-permute-start | bytes 983048 | tf_op jit(solution)/shard_map/ppermute | solution.py:771
  5.7 0.5 collective-permute-start.2
  6.2 8.6 %collective-permute-done.3.refs_1_ = bf16[128,1280]{1,0:T(8,128)(2,1)S(1)} collective-permute-done((bf16[128,1280]{1,0:T(8,128)(2,1)S(1)}, bf16[128,1280]{1,0:T(8,128)(2,1)S(1)}, u32[]{:S(2)}, u32[]{:S(2)}) %collective-permute-start.3) | collective-permute-done | bytes 327712 | tf_op jit(solution)/shard_map/ppermute | solution.py:771
  14.8 0.0 collective-permute-start.5
  14.8 5.9 %collective-permute-done.2.refs_0_ = bf16[128,1280]{1,0:T(8,128)(2,1)S(1)} collective-permute-done((bf16[128,1280]{1,0:T(8,128)(2,1)S(1)}, bf16[128,1280]{1,0:T(8,128)(2,1)S(1)}, u32[]{:S(2)}, u32[]{:S(2)}) %collective-permute-start.2) | collective-permute-done | bytes 327712 | tf_op jit(solution)/shard_map/ppermute | solution.py:771
  20.7 0.0 collective-permute-start.4
  20.7 3.4 %collective-permute-start = (s32[2]{0:T(128)S(1)}, s32[2]{0:T(128)S(1)}, u32[]{:S(2)}, u32[]{:S(2)}) collective-permute-start(s32[2]{0:T(128)S(1)} %get-tuple-element.38.mine), channel_id=1, source_target_pairs={{0,4},{2,6},{4,8},{5,1},{6,10},{7,3},{8,12},{9,5},{10,14},{11,7},{... | collective-permute-start | bytes 32 | tf_op jit(solution)/shard_map/ppermute | solution.py:772
  24.1 3.4 %collective-permute-start.7 = (bf16[128,1280]{1,0:T(8,128)(2,1)S(1)}, bf16[128,1280]{1,0:T(8,128)(2,1)S(1)}, u32[]{:S(2)}, u32[]{:S(2)}) collective-permute-start(bf16[128,1280]{1,0:T(8,128)(2,1)S(1)} %collective-permute-done.3.refs_1_), channel_id=1, source_target_pairs={{0,4},{1,5},{4,8},{5,9},{6,2},{7,3},{8,12},{9,13},{10,6},{11,7},{1... | collective-permute-start | bytes 983048 | tf_op jit(solution)/shard_map/ppermute | solution.py:781
  27.5 3.4 %collective-permute-start.6 = (bf16[128,1280]{1,0:T(8,128)(2,1)S(1)}, bf16[128,1280]{1,0:T(8,128)(2,1)S(1)}, u32[]{:S(2)}, u32[]{:S(2)}) collective-permute-start(bf16[128,1280]{1,0:T(8,128)(2,1)S(1)} %collective-permute-done.2.refs_0_), channel_id=1, source_target_pairs={{0,4},{1,5},{4,8},{5,9},{6,2},{7,3},{8,12},{9,13},{10,6},{11,7},{1... | collective-permute-start | bytes 983048 | tf_op jit(solution)/shard_map/ppermute | solution.py:781
  31.0 0.0 copy-start.3
  31.0 0.0 copy-start.4
  31.0 0.0 copy-start.5
  31.0 3.0 %own_project.2 = (bf16[1024,640]{1,0:T(8,128)(2,1)S(1)}, bf16[512,640]{1,0:T(8,128)(2,1)S(1)}, bf16[512,640]{1,0:T(8,128)(2,1)S(1)}) custom-call(bf16[512,1280]{1,0:T(8,128)(2,1)S(1)} %get-tuple-element.40.x_ref.own, bf16[1280,2688]{1,0:T(8,128)(2,1)S(1)} %get-tuple-element.41.weights.refs_4_), custom_call_target="tpu_custom_call" | custom-call | flops 2516582400 | bytes 4915200 | tf_op jit(solution)/shard_map/own_project/pallas_call | solution.py:226
  34.0 0.0 collective-permute-done.asked
  34.0 0.0 collective-permute-done.5.refs_3_
  34.0 0.0 collective-permute-done.4.refs_2_
  34.0 0.0 copy-done.3
  34.0 0.0 copy-done.4
  34.0 0.0 copy-done.5
  34.0 9.9 %attention.3 = (f32[512,640]{1,0:T(8,128)S(1)}, f32[512,640]{1,0:T(8,128)S(1)}, f32[512,640]{1,0:T(8,128)S(1)}, bf16[128,384]{1,0:T(8,128)(2,1)S(1)}) custom-call(s32[12]{0:T(128)S(1)} %copy-done.4, s32[4,4]{1,0:T(4,128)S(1)} %copy-done.3, s32[4]{0:T(128)S(1)} %copy-done.5, s32[2]{0:T(128)S(1)} %get-tuple-element.38.mine, s32[2]{0:T(128)S(1)} %get-tuple-element.39.yours, ...), custom_call_target="tpu_custom_call" | custom-call | flops 1342177280 | bytes 2621440 | tf_op jit(solution)/shard_map/attention/pallas_call | solution.py:512
  43.9 0.0 collective-permute-done.7.refs_5_.last.refs_1_
  43.9 0.0 collective-permute-done.6.refs_4_.refs_0_
  43.9 0.1 collective-permute-start.8
  44.0 0.5 collective-permute-start.9
  44.5 0.6 pick.2
  45.1 4.3 %collective-permute-start.1 = (bf16[128,1280]{1,0:T(8,128)(2,1)S(1)}, bf16[128,1280]{1,0:T(8,128)(2,1)S(1)}, u32[]{:S(2)}, u32[]{:S(2)}) collective-permute-start(bf16[128,1280]{1,0:T(8,128)(2,1)S(1)} %pick.2), channel_id=1, source_target_pairs={{1,5},{3,7},{4,0},{5,9},{6,2},{7,11},{8,4},{9,13},{10,6},{11,15},{... | collective-permute-start | bytes 983048 | tf_op jit(solution)/shard_map/ppermute | solution.py:778
  49.3 0.0 collective-permute-done.8.refs_6_.refs_2_
  49.3 0.0 collective-permute-done.9.refs_7_.last_s.refs_3_
  49.3 0.6 pick.3
  50.0 0.0 copy-start.2
  50.0 2.2 %collective-permute-start.10 = (bf16[128,1280]{1,0:T(8,128)(2,1)S(1)}, bf16[128,1280]{1,0:T(8,128)(2,1)S(1)}, u32[]{:S(2)}, u32[]{:S(2)}) collective-permute-start(bf16[128,1280]{1,0:T(8,128)(2,1)S(1)} %pick.3), channel_id=1, source_target_pairs={{1,5},{3,7},{4,0},{5,9},{6,2},{7,11},{8,4},{9,13},{10,6},{11,15},{... | collective-permute-start | bytes 983048 | tf_op jit(solution)/shard_map/ppermute | solution.py:797
  52.2 1.2 %own_project.3 = (bf16[512,384]{1,0:T(8,128)(2,1)S(1)}, bf16[512,384]{1,0:T(8,128)(2,1)S(1)}) custom-call(bf16[512,1280]{1,0:T(8,128)(2,1)S(1)} %get-tuple-element.40.x_ref.own, bf16[1280,2688]{1,0:T(8,128)(2,1)S(1)} %get-tuple-element.41.weights.refs_4_), custom_call_target="tpu_custom_call" | custom-call | flops 1006632960 | bytes 1966080 | tf_op jit(solution)/shard_map/own_project/pallas_call | solution.py:226
  53.4 0.0 copy-done.2
  53.4 8.9 %shard_map.127.refs_8_.refs_3_ = bf16[512,384]{1,0:T(8,128)(2,1)S(1)} custom-call(s32[12]{0:T(128)S(1)} %copy-done.4, bf16[512,384]{1,0:T(8,128)(2,1)S(1)} %get-tuple-element.53.own_ref, bf16[128,384]{1,0:T(8,128)(2,1)S(1)} %get-tuple-element.54.rim_p, bf16[128,1280]{1,0:T(8,128)(2,1)S(1)} %collective-permute-done.7.refs_5_.last.refs_1_, ...), custom_call_target="tpu_custom_call" | custom-call | flops 1006632960 | bytes 1572864 | tf_op jit(solution)/shard_map/pallas_call | solution.py:719
  62.3 0.0 copy-start
  62.3 0.0 copy-start.1
  62.3 0.0 collective-permute-done.1.refs_0_
  62.4 2.2 %collective-permute-done.10.refs_2_ = bf16[128,1280]{1,0:T(8,128)(2,1)S(1)} collective-permute-done((bf16[128,1280]{1,0:T(8,128)(2,1)S(1)}, bf16[128,1280]{1,0:T(8,128)(2,1)S(1)}, u32[]{:S(2)}, u32[]{:S(2)}) %collective-permute-start.10) | collective-permute-done | bytes 327712 | tf_op jit(solution)/shard_map/ppermute | solution.py:797
  64.6 0.0 collective-permute-start.11
  64.6 0.5 collective-permute-start.12
  65.1 1.9 %other_project.1 = (bf16[512,640]{1,0:T(8,128)(2,1)S(1)}, bf16[512,640]{1,0:T(8,128)(2,1)S(1)}) custom-call(bf16[128,1280]{1,0:T(8,128)(2,1)S(1)} %collective-permute-done.6.refs_4_.refs_0_, bf16[128,1280]{1,0:T(8,128)(2,1)S(1)} %collective-permute-done.7.refs_5_.last.refs_1_, bf16[128,1280]{1,0:T(8,128)(2,1)S(1)} %collective-permute-done.8.refs_6_.refs_2_, ...), custom_call_target="tpu_custom_call" | custom-call | flops 1677721600 | bytes 3276800 | tf_op jit(solution)/shard_map/other_project/pallas_call | solution.py:247
  67.0 0.0 collective-permute-done.11.refs_1_
  67.0 0.0 collective-permute-done.12.refs_3_
  67.0 0.0 copy-done
  67.0 0.0 copy-done.1
  67.0 7.1 %attention.4 = (bf16[256,1280]{1,0:T(8,128)(2,1)S(1)}, bf16[1024,640]{1,0:T(8,128)(2,1)S(1)}, bf16[1024,640]{1,0:T(8,128)(2,1)S(1)}) custom-call(s32[12]{0:T(128)S(1)} %copy-done.4, s32[4,4]{1,0:T(4,128)S(1)} %copy-done.3, s32[4]{0:T(128)S(1)} %copy-done.5, s32[2]{0:T(128)S(1)} %get-tuple-element.38.mine, s32[2]{0:T(128)S(1)} %get-tuple-element.39.yours, ...), custom_call_target="tpu_custom_call" | custom-call | flops 671088640 | bytes 2621440 | tf_op jit(solution)/shard_map/attention/pallas_call | solution.py:512
  74.1 1.0 %collective-permute-start.13 = (bf16[256,1280]{1,0:T(8,128)(2,1)S(1)}, bf16[256,1280]{1,0:T(8,128)(2,1)S(1)}, u32[]{:S(2)}, u32[]{:S(2)}) collective-permute-start(bf16[256,1280]{1,0:T(8,128)(2,1)S(1)} %get-tuple-element.70), channel_id=1, source_target_pairs={{0,1},{1,0},{2,3},{3,2},{4,5},{5,4},{6,7},{7,6},{8,9},{9,8},{10,11... | collective-permute-start | bytes 1966088 | tf_op jit(solution)/shard_map/ppermute | solution.py:35
  75.0 6.2 %attention.5 = f32[256,1280]{1,0:T(8,128)S(1)} custom-call(s32[12]{0:T(128)S(1)} %copy-done.4, s32[4,4]{1,0:T(4,128)S(1)} %copy-done.3, s32[4]{0:T(128)S(1)} %copy-done.5, s32[2]{0:T(128)S(1)} %get-tuple-element.38.mine, s32[2]{0:T(128)S(1)} %get-tuple-element.39.yours, bf16[1024,640]{1,0:T(8,128)(2,1)S(1)} %get-tuple-element.42.q_ref, ...), custom_call_target="tpu_custom_call" | custom-call | flops 671088640 | bytes 2621440 | tf_op jit(solution)/shard_map/attention/pallas_call | solution.py:512
  81.2 0.0 collective-permute-done.13
  81.2 1.0 %add_convert_fusion = bf16[256,1280]{1,0:T(8,128)(2,1)} fusion(f32[256,1280]{1,0:T(8,128)S(1)} %attention.5, bf16[256,1280]{1,0:T(8,128)(2,1)S(1)} %collective-permute-done.13), kind=kLoop, calls=%fused_computation | loop fusion | flops 983040 | bytes 2621440 | tf_op jit(solution)/shard_map/convert_element_type | solution.py:827
  (1 shorter events, 0.0 us)
Async XLA Ops:
  4.1 10.6 %collective-permute-start.3 = (bf16[128,1280]{1,0:T(8,128)(2,1)S(1)}, bf16[128,1280]{1,0:T(8,128)(2,1)S(1)}, u32[]{:S(2)}, u32[]{:S(2)}) collective-permute-start(bf16[128,1280]{1,0:T(8,128)(2,1)S(1)} %get-tuple-element.71), channel_id=1, source_target_pairs={{0,2},{1,3},{2,0},{3,1},{4,6},{5,7},{6,4},{7,5},{8,10},{9,11},{10,... | collective-permute-start | bytes 983048 | tf_op jit(solution)/shard_map/ppermute | solution.py:771
  5.7 15.0 %collective-permute-start.2 = (bf16[128,1280]{1,0:T(8,128)(2,1)S(1)}, bf16[128,1280]{1,0:T(8,128)(2,1)S(1)}, u32[]{:S(2)}, u32[]{:S(2)}) collective-permute-start(bf16[128,1280]{1,0:T(8,128)(2,1)S(1)} %get-tuple-element.72), channel_id=1, source_target_pairs={{0,2},{1,3},{2,0},{3,1},{4,6},{5,7},{6,4},{7,5},{8,10},{9,11},{10,... | collective-permute-start | bytes 983048 | tf_op jit(solution)/shard_map/ppermute | solution.py:771
  14.8 19.2 %collective-permute-start.5 = (bf16[128,1280]{1,0:T(8,128)(2,1)S(1)}, bf16[128,1280]{1,0:T(8,128)(2,1)S(1)}, u32[]{:S(2)}, u32[]{:S(2)}) collective-permute-start(bf16[128,1280]{1,0:T(8,128)(2,1)S(1)} %collective-permute-done.3.refs_1_), channel_id=1, source_target_pairs={{0,1},{1,0},{2,3},{3,2},{4,5},{5,4},{6,7},{7,6},{8,9},{9,8},{10,11... | collective-permute-start | bytes 983048 | tf_op jit(solution)/shard_map/ppermute | solution.py:35
  20.7 13.3 %collective-permute-start.4 = (bf16[128,1280]{1,0:T(8,128)(2,1)S(1)}, bf16[128,1280]{1,0:T(8,128)(2,1)S(1)}, u32[]{:S(2)}, u32[]{:S(2)}) collective-permute-start(bf16[128,1280]{1,0:T(8,128)(2,1)S(1)} %collective-permute-done.2.refs_0_), channel_id=1, source_target_pairs={{0,1},{1,0},{2,3},{3,2},{4,5},{5,4},{6,7},{7,6},{8,9},{9,8},{10,11... | collective-permute-start | bytes 983048 | tf_op jit(solution)/shard_map/ppermute | solution.py:35
  20.7 13.3 %collective-permute-start = (s32[2]{0:T(128)S(1)}, s32[2]{0:T(128)S(1)}, u32[]{:S(2)}, u32[]{:S(2)}) collective-permute-start(s32[2]{0:T(128)S(1)} %get-tuple-element.38.mine), channel_id=1, source_target_pairs={{0,4},{2,6},{4,8},{5,1},{6,10},{7,3},{8,12},{9,5},{10,14},{11,7},{... | collective-permute-start | bytes 32 | tf_op jit(solution)/shard_map/ppermute | solution.py:772
  24.1 19.8 %collective-permute-start.7 = (bf16[128,1280]{1,0:T(8,128)(2,1)S(1)}, bf16[128,1280]{1,0:T(8,128)(2,1)S(1)}, u32[]{:S(2)}, u32[]{:S(2)}) collective-permute-start(bf16[128,1280]{1,0:T(8,128)(2,1)S(1)} %collective-permute-done.3.refs_1_), channel_id=1, source_target_pairs={{0,4},{1,5},{4,8},{5,9},{6,2},{7,3},{8,12},{9,13},{10,6},{11,7},{1... | collective-permute-start | bytes 983048 | tf_op jit(solution)/shard_map/ppermute | solution.py:781
  27.5 16.4 %collective-permute-start.6 = (bf16[128,1280]{1,0:T(8,128)(2,1)S(1)}, bf16[128,1280]{1,0:T(8,128)(2,1)S(1)}, u32[]{:S(2)}, u32[]{:S(2)}) collective-permute-start(bf16[128,1280]{1,0:T(8,128)(2,1)S(1)} %collective-permute-done.2.refs_0_), channel_id=1, source_target_pairs={{0,4},{1,5},{4,8},{5,9},{6,2},{7,3},{8,12},{9,13},{10,6},{11,7},{1... | collective-permute-start | bytes 983048 | tf_op jit(solution)/shard_map/ppermute | solution.py:781
  31.0 3.0 %copy-start.3 = (s32[4,4]{1,0:T(4,128)S(1)}, s32[4,4]{1,0:T(4,128)}, u32[]{:S(2)}) copy-start(s32[4,4]{1,0:T(4,128)} %lists.5) | copy-start | bytes 196
  31.0 3.0 %copy-start.4 = (s32[12]{0:T(128)S(1)}, s32[12]{0:T(128)}, u32[]{:S(2)}) copy-start(s32[12]{0:T(128)} %starts.7) | copy-start | bytes 148
  31.0 3.0 %copy-start.5 = (s32[4]{0:T(128)S(1)}, s32[4]{0:T(128)}, u32[]{:S(2)}) copy-start(s32[4]{0:T(128)} %counts.5) | copy-start | bytes 52
  43.9 5.4 %collective-permute-start.8 = (bf16[128,1280]{1,0:T(8,128)(2,1)S(1)}, bf16[128,1280]{1,0:T(8,128)(2,1)S(1)}, u32[]{:S(2)}, u32[]{:S(2)}) collective-permute-start(bf16[128,1280]{1,0:T(8,128)(2,1)S(1)} %collective-permute-done.6.refs_4_.refs_0_), channel_id=1, source_target_pairs={{0,1},{1,0},{2,3},{3,2},{4,5},{5,4},{6,7},{7,6},{8,9},{9,8},{10,11... | collective-permute-start | bytes 983048 | tf_op jit(solution)/shard_map/ppermute | solution.py:35
  44.0 5.3 %collective-permute-start.9 = (bf16[128,1280]{1,0:T(8,128)(2,1)S(1)}, bf16[128,1280]{1,0:T(8,128)(2,1)S(1)}, u32[]{:S(2)}, u32[]{:S(2)}) collective-permute-start(bf16[128,1280]{1,0:T(8,128)(2,1)S(1)} %collective-permute-done.7.refs_5_.last.refs_1_), channel_id=1, source_target_pairs={{0,1},{1,0},{2,3},{3,2},{4,5},{5,4},{6,7},{7,6},{8,9},{9,8},{10,11... | collective-permute-start | bytes 983048 | tf_op jit(solution)/shard_map/ppermute | solution.py:35
  45.1 17.3 %collective-permute-start.1 = (bf16[128,1280]{1,0:T(8,128)(2,1)S(1)}, bf16[128,1280]{1,0:T(8,128)(2,1)S(1)}, u32[]{:S(2)}, u32[]{:S(2)}) collective-permute-start(bf16[128,1280]{1,0:T(8,128)(2,1)S(1)} %pick.2), channel_id=1, source_target_pairs={{1,5},{3,7},{4,0},{5,9},{6,2},{7,11},{8,4},{9,13},{10,6},{11,15},{... | collective-permute-start | bytes 983048 | tf_op jit(solution)/shard_map/ppermute | solution.py:778
  50.0 3.5 %copy-start.2 = (bf16[128,384]{1,0:T(8,128)(2,1)S(1)}, bf16[128,384]{1,0:T(8,128)(2,1)}, u32[]{:S(2)}) copy-start(bf16[128,384]{1,0:T(8,128)(2,1)} %taps_ref.1) | copy-start | bytes 294916
  50.0 14.6 %collective-permute-start.10 = (bf16[128,1280]{1,0:T(8,128)(2,1)S(1)}, bf16[128,1280]{1,0:T(8,128)(2,1)S(1)}, u32[]{:S(2)}, u32[]{:S(2)}) collective-permute-start(bf16[128,1280]{1,0:T(8,128)(2,1)S(1)} %pick.3), channel_id=1, source_target_pairs={{1,5},{3,7},{4,0},{5,9},{6,2},{7,11},{8,4},{9,13},{10,6},{11,15},{... | collective-permute-start | bytes 983048 | tf_op jit(solution)/shard_map/ppermute | solution.py:797
  62.3 4.7 %copy-start = (bf16[640,1280]{1,0:T(8,128)(2,1)S(1)}, bf16[640,1280]{1,0:T(8,128)(2,1)}, u32[]{:S(2)}) copy-start(bf16[640,1280]{1,0:T(8,128)(2,1)} %refs_4_.3) | copy-start | bytes 4915204
  62.3 4.7 %copy-start.1 = (bf16[384,1280]{1,0:T(8,128)(2,1)S(1)}, bf16[384,1280]{1,0:T(8,128)(2,1)}, u32[]{:S(2)}) copy-start(bf16[384,1280]{1,0:T(8,128)(2,1)} %refs_5_.1) | copy-start | bytes 2949124
  64.6 2.4 %collective-permute-start.11 = (bf16[128,1280]{1,0:T(8,128)(2,1)S(1)}, bf16[128,1280]{1,0:T(8,128)(2,1)S(1)}, u32[]{:S(2)}, u32[]{:S(2)}) collective-permute-start(bf16[128,1280]{1,0:T(8,128)(2,1)S(1)} %collective-permute-done.1.refs_0_), channel_id=1, source_target_pairs={{0,1},{1,0},{2,3},{3,2},{4,5},{5,4},{6,7},{7,6},{8,9},{9,8},{10,11... | collective-permute-start | bytes 983048 | tf_op jit(solution)/shard_map/ppermute | solution.py:35
  64.6 2.4 %collective-permute-start.12 = (bf16[128,1280]{1,0:T(8,128)(2,1)S(1)}, bf16[128,1280]{1,0:T(8,128)(2,1)S(1)}, u32[]{:S(2)}, u32[]{:S(2)}) collective-permute-start(bf16[128,1280]{1,0:T(8,128)(2,1)S(1)} %collective-permute-done.10.refs_2_), channel_id=1, source_target_pairs={{0,1},{1,0},{2,3},{3,2},{4,5},{5,4},{6,7},{7,6},{8,9},{9,8},{10,11... | collective-permute-start | bytes 983048 | tf_op jit(solution)/shard_map/ppermute | solution.py:35
  74.1 7.2 %collective-permute-start.13 = (bf16[256,1280]{1,0:T(8,128)(2,1)S(1)}, bf16[256,1280]{1,0:T(8,128)(2,1)S(1)}, u32[]{:S(2)}, u32[]{:S(2)}) collective-permute-start(bf16[256,1280]{1,0:T(8,128)(2,1)S(1)} %get-tuple-element.70), channel_id=1, source_target_pairs={{0,1},{1,0},{2,3},{3,2},{4,5},{5,4},{6,7},{7,6},{8,9},{9,8},{10,11... | collective-permute-start | bytes 1966088 | tf_op jit(solution)/shard_map/ppermute | solution.py:35

commit v3 on v2

--- a/solution.py
+++ b/solution.py
@@ -55,10 +55,10 @@
 PIECES = 4
 
 
-def plan_kernel(per_shard, nweights, lists_in, tokens, gain_in, *refs):
+def plan_kernel(per_shard, nweights, lists_in, counts_in, tokens, gain_in, *refs):
     weights, refs = refs[:nweights], refs[nweights:]
     mine, yours, normed, half, *refs = refs
-    every, lists, gain, rows, sem = refs
+    every, lists, counts, gain, rows, sem = refs
     kept, column = [], 0
     for w in weights:
         kept.append(every.at[:, pl.ds(column, w.shape[1])])
@@ -68,6 +68,7 @@
     small = [
         pltpu.make_async_copy(lists_in, lists, sem.at[PIECES]),
         pltpu.make_async_copy(gain_in, gain, sem.at[PIECES + 1]),
+        pltpu.make_async_copy(counts_in, counts, sem.at[PIECES + 2]),
     ]
     copies = [
         pltpu.make_async_copy(
@@ -76,7 +77,7 @@
         for n in range(PIECES)
     ]
     copies += [
-        pltpu.make_async_copy(weights[n], kept[n], sem.at[PIECES + 2 + n]) for n in range(nweights)
+        pltpu.make_async_copy(weights[n], kept[n], sem.at[PIECES + 3 + n]) for n in range(nweights)
     ]
     for copy in small + copies:
         copy.start()
@@ -101,7 +102,8 @@
         for q in range(per_shard):
             for m in range(NB):
                 local = lists[q, m] - low
-                found = jnp.where((local >= 0) & (local < per_shard), local, found)
+                named = (local >= 0) & (local < per_shard) & (m < counts[q])
+                found = jnp.where(named, local, found)
         return found
 
     side = 1 - 2 * core
@@ -114,7 +116,7 @@
         copy.wait()
 
 
-def plan(lists, tokens, gain, weights):
+def plan(lists, counts, tokens, gain, weights):
     rows, cols = tokens.shape
     pair = jax.ShapeDtypeStruct((2,), jnp.int32)
     return pl.pallas_call(
@@ -126,17 +128,18 @@
             jax.ShapeDtypeStruct((rows // 2, cols), BF16),
         ]
         + [jax.ShapeDtypeStruct((cols, sum(w.shape[1] for w in weights)), BF16)],
-        in_specs=[ANY] * (3 + len(weights)),
+        in_specs=[ANY] * (4 + len(weights)),
         out_specs=[SMEM, SMEM] + [VMEM] * 3,
         scratch_shapes=[
             pltpu.SMEM(lists.shape, jnp.int32),
+            pltpu.SMEM(counts.shape, jnp.int32),
             pltpu.VMEM(gain.shape, F32),
             pltpu.VMEM((rows, cols), BF16),
-            pltpu.SemaphoreType.DMA((PIECES + 2 + len(weights),)),
+            pltpu.SemaphoreType.DMA((PIECES + 3 + len(weights),)),
         ],
         compiler_params=limit(14),
         name="plan",
-    )(in_hbm(lists), in_hbm(tokens), in_hbm(gain), *[in_hbm(w) for w in weights])
+    )(in_hbm(lists), in_hbm(counts), in_hbm(tokens), in_hbm(gain), *[in_hbm(w) for w in weights])
 
 
 def pick_own_kernel(asked, own, out):
@@ -759,7 +762,7 @@
     head_cols, channels = w_query.shape[1], conv_in_w.shape[1]
     kv_columns, conv_columns = head_cols, 3 * head_cols
     mine, yours, normed, half, weights = plan(
-        block_lists, tokens, norm_gain, (w_query, w_key, w_value, conv_in_w, conv_gate_w)
+        block_lists, block_counts, tokens, norm_gain, (w_query, w_key, w_value, conv_in_w, conv_gate_w)
     )
     to_asking = flat_pairs(shards, lambda i, h: i + (-2 if h == 0 else 2))
     to_asked = flat_pairs(shards, lambda i, h: i + (2 if h == 0 else -2))

time: 82.5 us -> 82.4 us (level)
  no operation moved by 1% of the time
where the time goes in v3:
time: 82.4 us; the launch traced here: 82.2 us
  Pallas kernels  43.2 us (52%)
  starting transfers between devices  20.9 us (25%)
  waiting for transfers between devices  16.7 us (20%)
  other arithmetic  0.95 us (1%)
    pallas_call x3, Pallas kernels, attention(): pl.pallas_call(functools.partial(attention_kernel, stage, columns, len(ne...  23.1 us
    ppermute x2, waiting for transfers between devices, body(): partner[n] = lax.ppermute(chunks[n], AXES, to_partner)  14.4 us
    pallas_call x1, Pallas kernels, convolution(): pl.pallas_call(functools.partial(conv_kernel, starts.shape[0], columns),...  8.89 us
    ppermute x2, starting transfers between devices, body(): other[n] = lax.ppermute(partner[n], AXES, to_other)  6.86 us
    ppermute x1, starting transfers between devices, body(): far = lax.ppermute(picked, AXES, to_asking)  4.25 us
    pallas_call x2, Pallas kernels, own_project(): pl.pallas_call(functools.partial(own_kernel, columns, scale), out_shape=o...  4.15 us
    pallas_call x1, Pallas kernels, plan(): pl.pallas_call(functools.partial(plan_kernel, rows // BLK, len(weights)),...  4.07 us
    ppermute x1, starting transfers between devices, body(): asked = lax.ppermute(mine, AXES, to_asked)  3.42 us
  transfers between devices with their start and end apart: 14, of which 3 were waited for; matrix products, arithmetic and copies ran while one was open for 0% of the time, Pallas kernels for 39%

profile of v3, /device:TPU:16, one launch (start us, length us, event | category | flops | bytes accessed | tf_op | source)
XLA Modules:
  0.0 82.2 jit_solution(980370441707753603)
XLA Ops:
  0.0 4.1 %plan.1 = (s32[2]{0:T(128)S(1)}, s32[2]{0:T(128)S(1)}, bf16[512,1280]{1,0:T(8,128)(2,1)S(1)}, bf16[256,1280]{1,0:T(8,128)(2,1)S(1)}, bf16[1280,2688]{1,0:T(8,128)(2,1)S(1)}) custom-call(s32[4,4]{1,0:T(4,128)} %lists.5, s32[4]{0:T(128)} %counts.5, bf16[512,1280]{1,0:T(8,128)(2,1)} %tokens.1, f32[1280]{0:T(1024)} %gain_in.1, bf16[1280,640]{1,0:T(8,128)(2,1)} %refs_0_.1, ...), custom_call_target="tpu_custom_call" | custom-call | tf_op jit(solution)/shard_map/plan/pallas_call | solution.py:122
  4.1 1.6 %collective-permute-start.3 = (bf16[128,1280]{1,0:T(8,128)(2,1)S(1)}, bf16[128,1280]{1,0:T(8,128)(2,1)S(1)}, u32[]{:S(2)}, u32[]{:S(2)}) collective-permute-start(bf16[128,1280]{1,0:T(8,128)(2,1)S(1)} %get-tuple-element.71), channel_id=1, source_target_pairs={{0,2},{1,3},{2,0},{3,1},{4,6},{5,7},{6,4},{7,5},{8,10},{9,11},{10,... | collective-permute-start | bytes 983048 | tf_op jit(solution)/shard_map/ppermute | solution.py:774
  5.7 0.5 collective-permute-start.2
  6.2 8.6 %collective-permute-done.3.refs_1_ = bf16[128,1280]{1,0:T(8,128)(2,1)S(1)} collective-permute-done((bf16[128,1280]{1,0:T(8,128)(2,1)S(1)}, bf16[128,1280]{1,0:T(8,128)(2,1)S(1)}, u32[]{:S(2)}, u32[]{:S(2)}) %collective-permute-start.3) | collective-permute-done | bytes 327712 | tf_op jit(solution)/shard_map/ppermute | solution.py:774
  14.8 0.0 collective-permute-start.5
  14.8 5.9 %collective-permute-done.2.refs_0_ = bf16[128,1280]{1,0:T(8,128)(2,1)S(1)} collective-permute-done((bf16[128,1280]{1,0:T(8,128)(2,1)S(1)}, bf16[128,1280]{1,0:T(8,128)(2,1)S(1)}, u32[]{:S(2)}, u32[]{:S(2)}) %collective-permute-start.2) | collective-permute-done | bytes 327712 | tf_op jit(solution)/shard_map/ppermute | solution.py:774
  20.7 0.0 collective-permute-start.4
  20.7 3.4 %collective-permute-start = (s32[2]{0:T(128)S(1)}, s32[2]{0:T(128)S(1)}, u32[]{:S(2)}, u32[]{:S(2)}) collective-permute-start(s32[2]{0:T(128)S(1)} %get-tuple-element.38.mine), channel_id=1, source_target_pairs={{0,4},{2,6},{4,8},{5,1},{6,10},{7,3},{8,12},{9,5},{10,14},{11,7},{... | collective-permute-start | bytes 32 | tf_op jit(solution)/shard_map/ppermute | solution.py:775
  24.1 3.4 %collective-permute-start.7 = (bf16[128,1280]{1,0:T(8,128)(2,1)S(1)}, bf16[128,1280]{1,0:T(8,128)(2,1)S(1)}, u32[]{:S(2)}, u32[]{:S(2)}) collective-permute-start(bf16[128,1280]{1,0:T(8,128)(2,1)S(1)} %collective-permute-done.3.refs_1_), channel_id=1, source_target_pairs={{0,4},{1,5},{4,8},{5,9},{6,2},{7,3},{8,12},{9,13},{10,6},{11,7},{1... | collective-permute-start | bytes 983048 | tf_op jit(solution)/shard_map/ppermute | solution.py:784
  27.5 3.4 %collective-permute-start.6 = (bf16[128,1280]{1,0:T(8,128)(2,1)S(1)}, bf16[128,1280]{1,0:T(8,128)(2,1)S(1)}, u32[]{:S(2)}, u32[]{:S(2)}) collective-permute-start(bf16[128,1280]{1,0:T(8,128)(2,1)S(1)} %collective-permute-done.2.refs_0_), channel_id=1, source_target_pairs={{0,4},{1,5},{4,8},{5,9},{6,2},{7,3},{8,12},{9,13},{10,6},{11,7},{1... | collective-permute-start | bytes 983048 | tf_op jit(solution)/shard_map/ppermute | solution.py:784
  31.0 0.0 copy-start.3
  31.0 0.0 copy-start.4
  31.0 0.0 copy-start.5
  31.0 3.0 %own_project.2 = (bf16[1024,640]{1,0:T(8,128)(2,1)S(1)}, bf16[512,640]{1,0:T(8,128)(2,1)S(1)}, bf16[512,640]{1,0:T(8,128)(2,1)S(1)}) custom-call(bf16[512,1280]{1,0:T(8,128)(2,1)S(1)} %get-tuple-element.40.x_ref.own, bf16[1280,2688]{1,0:T(8,128)(2,1)S(1)} %get-tuple-element.41.weights.refs_4_), custom_call_target="tpu_custom_call" | custom-call | flops 2516582400 | bytes 4915200 | tf_op jit(solution)/shard_map/own_project/pallas_call | solution.py:229
  34.0 0.0 collective-permute-done.asked
  34.0 0.0 collective-permute-done.5.refs_3_
  34.0 0.0 collective-permute-done.4.refs_2_
  34.0 0.0 copy-done.3
  34.0 0.0 copy-done.4
  34.0 0.0 copy-done.5
  34.0 9.8 %attention.3 = (f32[512,640]{1,0:T(8,128)S(1)}, f32[512,640]{1,0:T(8,128)S(1)}, f32[512,640]{1,0:T(8,128)S(1)}, bf16[128,384]{1,0:T(8,128)(2,1)S(1)}) custom-call(s32[12]{0:T(128)S(1)} %copy-done.4, s32[4,4]{1,0:T(4,128)S(1)} %copy-done.3, s32[4]{0:T(128)S(1)} %copy-done.5, s32[2]{0:T(128)S(1)} %get-tuple-element.38.mine, s32[2]{0:T(128)S(1)} %get-tuple-element.39.yours, ...), custom_call_target="tpu_custom_call" | custom-call | flops 1342177280 | bytes 2621440 | tf_op jit(solution)/shard_map/attention/pallas_call | solution.py:515
  43.9 0.0 collective-permute-done.7.refs_5_.last.refs_1_
  43.9 0.0 collective-permute-done.6.refs_4_.refs_0_
  43.9 0.1 collective-permute-start.8
  44.0 0.5 collective-permute-start.9
  44.5 0.6 pick.2
  45.0 4.3 %collective-permute-start.1 = (bf16[128,1280]{1,0:T(8,128)(2,1)S(1)}, bf16[128,1280]{1,0:T(8,128)(2,1)S(1)}, u32[]{:S(2)}, u32[]{:S(2)}) collective-permute-start(bf16[128,1280]{1,0:T(8,128)(2,1)S(1)} %pick.2), channel_id=1, source_target_pairs={{1,5},{3,7},{4,0},{5,9},{6,2},{7,11},{8,4},{9,13},{10,6},{11,15},{... | collective-permute-start | bytes 983048 | tf_op jit(solution)/shard_map/ppermute | solution.py:781
  49.3 0.0 collective-permute-done.8.refs_6_.refs_2_
  49.3 0.0 collective-permute-done.9.refs_7_.last_s.refs_3_
  49.3 0.6 pick.3
  49.9 0.0 copy-start.2
  49.9 2.2 %collective-permute-start.10 = (bf16[128,1280]{1,0:T(8,128)(2,1)S(1)}, bf16[128,1280]{1,0:T(8,128)(2,1)S(1)}, u32[]{:S(2)}, u32[]{:S(2)}) collective-permute-start(bf16[128,1280]{1,0:T(8,128)(2,1)S(1)} %pick.3), channel_id=1, source_target_pairs={{1,5},{3,7},{4,0},{5,9},{6,2},{7,11},{8,4},{9,13},{10,6},{11,15},{... | collective-permute-start | bytes 983048 | tf_op jit(solution)/shard_map/ppermute | solution.py:800
  52.2 1.2 %own_project.3 = (bf16[512,384]{1,0:T(8,128)(2,1)S(1)}, bf16[512,384]{1,0:T(8,128)(2,1)S(1)}) custom-call(bf16[512,1280]{1,0:T(8,128)(2,1)S(1)} %get-tuple-element.40.x_ref.own, bf16[1280,2688]{1,0:T(8,128)(2,1)S(1)} %get-tuple-element.41.weights.refs_4_), custom_call_target="tpu_custom_call" | custom-call | flops 1006632960 | bytes 1966080 | tf_op jit(solution)/shard_map/own_project/pallas_call | solution.py:229
  53.4 0.0 copy-done.2
  53.4 8.9 %shard_map.127.refs_8_.refs_3_ = bf16[512,384]{1,0:T(8,128)(2,1)S(1)} custom-call(s32[12]{0:T(128)S(1)} %copy-done.4, bf16[512,384]{1,0:T(8,128)(2,1)S(1)} %get-tuple-element.53.own_ref, bf16[128,384]{1,0:T(8,128)(2,1)S(1)} %get-tuple-element.54.rim_p, bf16[128,1280]{1,0:T(8,128)(2,1)S(1)} %collective-permute-done.7.refs_5_.last.refs_1_, ...), custom_call_target="tpu_custom_call" | custom-call | flops 1006632960 | bytes 1572864 | tf_op jit(solution)/shard_map/pallas_call | solution.py:722
  62.3 0.0 copy-start
  62.3 0.0 copy-start.1
  62.3 0.0 collective-permute-done.1.refs_0_
  62.3 2.2 %collective-permute-done.10.refs_2_ = bf16[128,1280]{1,0:T(8,128)(2,1)S(1)} collective-permute-done((bf16[128,1280]{1,0:T(8,128)(2,1)S(1)}, bf16[128,1280]{1,0:T(8,128)(2,1)S(1)}, u32[]{:S(2)}, u32[]{:S(2)}) %collective-permute-start.10) | collective-permute-done | bytes 327712 | tf_op jit(solution)/shard_map/ppermute | solution.py:800
  64.5 0.0 collective-permute-start.11
  64.5 0.5 collective-permute-start.12
  65.0 1.9 %other_project.1 = (bf16[512,640]{1,0:T(8,128)(2,1)S(1)}, bf16[512,640]{1,0:T(8,128)(2,1)S(1)}) custom-call(bf16[128,1280]{1,0:T(8,128)(2,1)S(1)} %collective-permute-done.6.refs_4_.refs_0_, bf16[128,1280]{1,0:T(8,128)(2,1)S(1)} %collective-permute-done.7.refs_5_.last.refs_1_, bf16[128,1280]{1,0:T(8,128)(2,1)S(1)} %collective-permute-done.8.refs_6_.refs_2_, ...), custom_call_target="tpu_custom_call" | custom-call | flops 1677721600 | bytes 3276800 | tf_op jit(solution)/shard_map/other_project/pallas_call | solution.py:250
  66.9 0.0 collective-permute-done.11.refs_1_
  66.9 0.0 collective-permute-done.12.refs_3_
  66.9 0.0 copy-done
  67.0 0.0 copy-done.1
  67.0 7.0 %attention.4 = (bf16[256,1280]{1,0:T(8,128)(2,1)S(1)}, bf16[1024,640]{1,0:T(8,128)(2,1)S(1)}, bf16[1024,640]{1,0:T(8,128)(2,1)S(1)}) custom-call(s32[12]{0:T(128)S(1)} %copy-done.4, s32[4,4]{1,0:T(4,128)S(1)} %copy-done.3, s32[4]{0:T(128)S(1)} %copy-done.5, s32[2]{0:T(128)S(1)} %get-tuple-element.38.mine, s32[2]{0:T(128)S(1)} %get-tuple-element.39.yours, ...), custom_call_target="tpu_custom_call" | custom-call | flops 671088640 | bytes 2621440 | tf_op jit(solution)/shard_map/attention/pallas_call | solution.py:515
  74.0 1.0 %collective-permute-start.13 = (bf16[256,1280]{1,0:T(8,128)(2,1)S(1)}, bf16[256,1280]{1,0:T(8,128)(2,1)S(1)}, u32[]{:S(2)}, u32[]{:S(2)}) collective-permute-start(bf16[256,1280]{1,0:T(8,128)(2,1)S(1)} %get-tuple-element.70), channel_id=1, source_target_pairs={{0,1},{1,0},{2,3},{3,2},{4,5},{5,4},{6,7},{7,6},{8,9},{9,8},{10,11... | collective-permute-start | bytes 1966088 | tf_op jit(solution)/shard_map/ppermute | solution.py:35
  75.0 6.2 %attention.5 = f32[256,1280]{1,0:T(8,128)S(1)} custom-call(s32[12]{0:T(128)S(1)} %copy-done.4, s32[4,4]{1,0:T(4,128)S(1)} %copy-done.3, s32[4]{0:T(128)S(1)} %copy-done.5, s32[2]{0:T(128)S(1)} %get-tuple-element.38.mine, s32[2]{0:T(128)S(1)} %get-tuple-element.39.yours, bf16[1024,640]{1,0:T(8,128)(2,1)S(1)} %get-tuple-element.42.q_ref, ...), custom_call_target="tpu_custom_call" | custom-call | flops 671088640 | bytes 2621440 | tf_op jit(solution)/shard_map/attention/pallas_call | solution.py:515
  81.2 0.0 collective-permute-done.13
  81.2 1.0 %add_convert_fusion = bf16[256,1280]{1,0:T(8,128)(2,1)} fusion(f32[256,1280]{1,0:T(8,128)S(1)} %attention.5, bf16[256,1280]{1,0:T(8,128)(2,1)S(1)} %collective-permute-done.13), kind=kLoop, calls=%fused_computation | loop fusion | flops 983040 | bytes 2621440 | tf_op jit(solution)/shard_map/convert_element_type | solution.py:830
  (1 shorter events, 0.0 us)
Async XLA Ops:
  4.1 10.6 %collective-permute-start.3 = (bf16[128,1280]{1,0:T(8,128)(2,1)S(1)}, bf16[128,1280]{1,0:T(8,128)(2,1)S(1)}, u32[]{:S(2)}, u32[]{:S(2)}) collective-permute-start(bf16[128,1280]{1,0:T(8,128)(2,1)S(1)} %get-tuple-element.71), channel_id=1, source_target_pairs={{0,2},{1,3},{2,0},{3,1},{4,6},{5,7},{6,4},{7,5},{8,10},{9,11},{10,... | collective-permute-start | bytes 983048 | tf_op jit(solution)/shard_map/ppermute | solution.py:774
  5.7 15.0 %collective-permute-start.2 = (bf16[128,1280]{1,0:T(8,128)(2,1)S(1)}, bf16[128,1280]{1,0:T(8,128)(2,1)S(1)}, u32[]{:S(2)}, u32[]{:S(2)}) collective-permute-start(bf16[128,1280]{1,0:T(8,128)(2,1)S(1)} %get-tuple-element.72), channel_id=1, source_target_pairs={{0,2},{1,3},{2,0},{3,1},{4,6},{5,7},{6,4},{7,5},{8,10},{9,11},{10,... | collective-permute-start | bytes 983048 | tf_op jit(solution)/shard_map/ppermute | solution.py:774
  14.8 19.2 %collective-permute-start.5 = (bf16[128,1280]{1,0:T(8,128)(2,1)S(1)}, bf16[128,1280]{1,0:T(8,128)(2,1)S(1)}, u32[]{:S(2)}, u32[]{:S(2)}) collective-permute-start(bf16[128,1280]{1,0:T(8,128)(2,1)S(1)} %collective-permute-done.3.refs_1_), channel_id=1, source_target_pairs={{0,1},{1,0},{2,3},{3,2},{4,5},{5,4},{6,7},{7,6},{8,9},{9,8},{10,11... | collective-permute-start | bytes 983048 | tf_op jit(solution)/shard_map/ppermute | solution.py:35
  20.7 13.3 %collective-permute-start.4 = (bf16[128,1280]{1,0:T(8,128)(2,1)S(1)}, bf16[128,1280]{1,0:T(8,128)(2,1)S(1)}, u32[]{:S(2)}, u32[]{:S(2)}) collective-permute-start(bf16[128,1280]{1,0:T(8,128)(2,1)S(1)} %collective-permute-done.2.refs_0_), channel_id=1, source_target_pairs={{0,1},{1,0},{2,3},{3,2},{4,5},{5,4},{6,7},{7,6},{8,9},{9,8},{10,11... | collective-permute-start | bytes 983048 | tf_op jit(solution)/shard_map/ppermute | solution.py:35
  20.7 13.3 %collective-permute-start = (s32[2]{0:T(128)S(1)}, s32[2]{0:T(128)S(1)}, u32[]{:S(2)}, u32[]{:S(2)}) collective-permute-start(s32[2]{0:T(128)S(1)} %get-tuple-element.38.mine), channel_id=1, source_target_pairs={{0,4},{2,6},{4,8},{5,1},{6,10},{7,3},{8,12},{9,5},{10,14},{11,7},{... | collective-permute-start | bytes 32 | tf_op jit(solution)/shard_map/ppermute | solution.py:775
  24.1 19.8 %collective-permute-start.7 = (bf16[128,1280]{1,0:T(8,128)(2,1)S(1)}, bf16[128,1280]{1,0:T(8,128)(2,1)S(1)}, u32[]{:S(2)}, u32[]{:S(2)}) collective-permute-start(bf16[128,1280]{1,0:T(8,128)(2,1)S(1)} %collective-permute-done.3.refs_1_), channel_id=1, source_target_pairs={{0,4},{1,5},{4,8},{5,9},{6,2},{7,3},{8,12},{9,13},{10,6},{11,7},{1... | collective-permute-start | bytes 983048 | tf_op jit(solution)/shard_map/ppermute | solution.py:784
  27.5 16.3 %collective-permute-start.6 = (bf16[128,1280]{1,0:T(8,128)(2,1)S(1)}, bf16[128,1280]{1,0:T(8,128)(2,1)S(1)}, u32[]{:S(2)}, u32[]{:S(2)}) collective-permute-start(bf16[128,1280]{1,0:T(8,128)(2,1)S(1)} %collective-permute-done.2.refs_0_), channel_id=1, source_target_pairs={{0,4},{1,5},{4,8},{5,9},{6,2},{7,3},{8,12},{9,13},{10,6},{11,7},{1... | collective-permute-start | bytes 983048 | tf_op jit(solution)/shard_map/ppermute | solution.py:784
  31.0 3.0 %copy-start.3 = (s32[4,4]{1,0:T(4,128)S(1)}, s32[4,4]{1,0:T(4,128)}, u32[]{:S(2)}) copy-start(s32[4,4]{1,0:T(4,128)} %lists.5) | copy-start | bytes 196
  31.0 3.0 %copy-start.4 = (s32[12]{0:T(128)S(1)}, s32[12]{0:T(128)}, u32[]{:S(2)}) copy-start(s32[12]{0:T(128)} %starts.7) | copy-start | bytes 148
  31.0 3.0 %copy-start.5 = (s32[4]{0:T(128)S(1)}, s32[4]{0:T(128)}, u32[]{:S(2)}) copy-start(s32[4]{0:T(128)} %counts.5) | copy-start | bytes 52
  43.9 5.4 %collective-permute-start.8 = (bf16[128,1280]{1,0:T(8,128)(2,1)S(1)}, bf16[128,1280]{1,0:T(8,128)(2,1)S(1)}, u32[]{:S(2)}, u32[]{:S(2)}) collective-permute-start(bf16[128,1280]{1,0:T(8,128)(2,1)S(1)} %collective-permute-done.6.refs_4_.refs_0_), channel_id=1, source_target_pairs={{0,1},{1,0},{2,3},{3,2},{4,5},{5,4},{6,7},{7,6},{8,9},{9,8},{10,11... | collective-permute-start | bytes 983048 | tf_op jit(solution)/shard_map/ppermute | solution.py:35
  44.0 5.3 %collective-permute-start.9 = (bf16[128,1280]{1,0:T(8,128)(2,1)S(1)}, bf16[128,1280]{1,0:T(8,128)(2,1)S(1)}, u32[]{:S(2)}, u32[]{:S(2)}) collective-permute-start(bf16[128,1280]{1,0:T(8,128)(2,1)S(1)} %collective-permute-done.7.refs_5_.last.refs_1_), channel_id=1, source_target_pairs={{0,1},{1,0},{2,3},{3,2},{4,5},{5,4},{6,7},{7,6},{8,9},{9,8},{10,11... | collective-permute-start | bytes 983048 | tf_op jit(solution)/shard_map/ppermute | solution.py:35
  45.0 17.3 %collective-permute-start.1 = (bf16[128,1280]{1,0:T(8,128)(2,1)S(1)}, bf16[128,1280]{1,0:T(8,128)(2,1)S(1)}, u32[]{:S(2)}, u32[]{:S(2)}) collective-permute-start(bf16[128,1280]{1,0:T(8,128)(2,1)S(1)} %pick.2), channel_id=1, source_target_pairs={{1,5},{3,7},{4,0},{5,9},{6,2},{7,11},{8,4},{9,13},{10,6},{11,15},{... | collective-permute-start | bytes 983048 | tf_op jit(solution)/shard_map/ppermute | solution.py:781
  49.9 3.5 %copy-start.2 = (bf16[128,384]{1,0:T(8,128)(2,1)S(1)}, bf16[128,384]{1,0:T(8,128)(2,1)}, u32[]{:S(2)}) copy-start(bf16[128,384]{1,0:T(8,128)(2,1)} %taps_ref.1) | copy-start | bytes 294916
  49.9 14.6 %collective-permute-start.10 = (bf16[128,1280]{1,0:T(8,128)(2,1)S(1)}, bf16[128,1280]{1,0:T(8,128)(2,1)S(1)}, u32[]{:S(2)}, u32[]{:S(2)}) collective-permute-start(bf16[128,1280]{1,0:T(8,128)(2,1)S(1)} %pick.3), channel_id=1, source_target_pairs={{1,5},{3,7},{4,0},{5,9},{6,2},{7,11},{8,4},{9,13},{10,6},{11,15},{... | collective-permute-start | bytes 983048 | tf_op jit(solution)/shard_map/ppermute | solution.py:800
  62.3 4.7 %copy-start = (bf16[640,1280]{1,0:T(8,128)(2,1)S(1)}, bf16[640,1280]{1,0:T(8,128)(2,1)}, u32[]{:S(2)}) copy-start(bf16[640,1280]{1,0:T(8,128)(2,1)} %refs_4_.3) | copy-start | bytes 4915204
  62.3 4.7 %copy-start.1 = (bf16[384,1280]{1,0:T(8,128)(2,1)S(1)}, bf16[384,1280]{1,0:T(8,128)(2,1)}, u32[]{:S(2)}) copy-start(bf16[384,1280]{1,0:T(8,128)(2,1)} %refs_5_.1) | copy-start | bytes 2949124
  64.5 2.4 %collective-permute-start.11 = (bf16[128,1280]{1,0:T(8,128)(2,1)S(1)}, bf16[128,1280]{1,0:T(8,128)(2,1)S(1)}, u32[]{:S(2)}, u32[]{:S(2)}) collective-permute-start(bf16[128,1280]{1,0:T(8,128)(2,1)S(1)} %collective-permute-done.1.refs_0_), channel_id=1, source_target_pairs={{0,1},{1,0},{2,3},{3,2},{4,5},{5,4},{6,7},{7,6},{8,9},{9,8},{10,11... | collective-permute-start | bytes 983048 | tf_op jit(solution)/shard_map/ppermute | solution.py:35
  64.5 2.4 %collective-permute-start.12 = (bf16[128,1280]{1,0:T(8,128)(2,1)S(1)}, bf16[128,1280]{1,0:T(8,128)(2,1)S(1)}, u32[]{:S(2)}, u32[]{:S(2)}) collective-permute-start(bf16[128,1280]{1,0:T(8,128)(2,1)S(1)} %collective-permute-done.10.refs_2_), channel_id=1, source_target_pairs={{0,1},{1,0},{2,3},{3,2},{4,5},{5,4},{6,7},{7,6},{8,9},{9,8},{10,11... | collective-permute-start | bytes 983048 | tf_op jit(solution)/shard_map/ppermute | solution.py:35
  74.0 7.2 %collective-permute-start.13 = (bf16[256,1280]{1,0:T(8,128)(2,1)S(1)}, bf16[256,1280]{1,0:T(8,128)(2,1)S(1)}, u32[]{:S(2)}, u32[]{:S(2)}) collective-permute-start(bf16[256,1280]{1,0:T(8,128)(2,1)S(1)} %get-tuple-element.70), channel_id=1, source_target_pairs={{0,1},{1,0},{2,3},{3,2},{4,5},{5,4},{6,7},{7,6},{8,9},{9,8},{10,11... | collective-permute-start | bytes 1966088 | tf_op jit(solution)/shard_map/ppermute | solution.py:35
